TPU v7x, 32 devices: a whole 2x2x4 slice. The times are simulated.
32 devices in a mesh: dp: 2 (over x), row: 4 (over y, core), col: 4 (over z).
Axes of the slice: x: 2, y: 2, z: 4, core: 2. Of those that a mesh axis runs over, the one named last changes fastest.
Arguments:
- inputs: bfloat16 [4096, 576], P(('dp', 'col'), 'row'), may hold values from -10 to 10
- first_gain: float32 [576], P('row'), may hold values from 0.25 to 1.75
- query_weight: bfloat16 [576, 576], P('row', 'col'), may hold values from -0.25 to 0.25
- key_matrix: bfloat16 [576, 192], P('row', 'col'), may hold values from -0.25 to 0.25
- value_matrix: bfloat16 [576, 192], P('row', 'col'), may hold values from -0.25 to 0.25
- output_weight: bfloat16 [576, 576], P('col', 'row'), may hold values from -1.5 to 1.5
- second_gain: float32 [576], P('row'), may hold values from 0.25 to 1.75
- gate_weight: bfloat16 [576, 1536], P('row', 'col'), may hold values from -0.25 to 0.25
- up_weight: bfloat16 [576, 1536], P('row', 'col'), may hold values from -0.25 to 0.25
- down_weight: bfloat16 [1536, 576], P('col', 'row'), may hold values from -0.15625 to 0.15625
- cotangent: bfloat16 [4096, 576], P(('dp', 'col'), 'row'), may hold values from -6 to 6
Outputs:
- result: bfloat16 [4096, 576], P(('dp', 'col'), 'row')
- input_grad: bfloat16 [4096, 576], P(('dp', 'col'), 'row')
- first_gain_grad: float32 [576], P('row')
- query_grad: float32 [576, 576], P('row', 'col')
- key_grad: float32 [576, 192], P('row', 'col')
- value_grad: float32 [576, 192], P('row', 'col')
- output_grad: float32 [576, 576], P('col', 'row')
- second_gain_grad: float32 [576], P('row')
- gate_grad: float32 [576, 1536], P('row', 'col')
- up_grad: float32 [576, 1536], P('row', 'col')
- down_grad: float32 [1536, 576], P('col', 'row')
All inputs are finite; a program needn't handle non-finite values.
Results may differ from a plain program's by a relative error of at most 0.035.
Values may be sent and summed in bfloat16 or wider, within the bound.
A program may use at most 64 MiB of HBM per device.

v0:
```python
import math

import jax
import jax.numpy as jnp
from jax import lax
from jax.sharding import PartitionSpec as P

QUERY_HEADS = 9
KEY_VALUE_HEADS = 3
HEAD_SIZE = 64
SEQUENCE_LENGTH = 2048


EPS = 1e-05
THETA = 100000.0
NEGATIVE_FILL = -1e30


def feature_sums(values):
    return lax.psum(values, "row")


def norm_forward(source, norm_gain):
    feature_total = source.shape[1] * lax.axis_size("row")
    norm_scale = lax.rsqrt(feature_sums(jnp.sum(source * source, axis=1)) / feature_total + EPS)[
        :, None
    ]
    return (norm_scale, (source * norm_scale * norm_gain).astype(jnp.bfloat16))


def norm_backward(source, norm_scale, norm_gain, upstream):
    feature_total = source.shape[1] * lax.axis_size("row")
    inner = feature_sums(jnp.sum(upstream * norm_gain * source, axis=1))[:, None]
    cubed = norm_scale * norm_scale * norm_scale
    d_source = norm_scale * norm_gain * upstream - source * cubed * inner / feature_total
    d_gain = jnp.sum(upstream * source * norm_scale, axis=0)
    return (d_source, d_gain)


def contract_rows(left, right):
    return lax.dot_general(
        left, right, (((0,), (0,)), ((), ())), preferred_element_type=jnp.float32
    )


def rows_project(values, weight):
    gathered = lax.all_gather(values, "col", axis=0, tiled=True)
    return (
        lax.psum_scatter(
            jnp.dot(gathered, weight, preferred_element_type=jnp.float32).astype(jnp.bfloat16),
            "row",
            scatter_dimension=0,
            tiled=True,
        ).astype(jnp.float32),
        gathered,
    )


def cols_project(values, weight):
    gathered = lax.all_gather(values, "row", axis=0, tiled=True)
    return (
        lax.psum_scatter(
            jnp.dot(gathered, weight, preferred_element_type=jnp.float32).astype(jnp.bfloat16),
            "col",
            scatter_dimension=0,
            tiled=True,
        ).astype(jnp.float32),
        gathered,
    )


def head_layout(values):
    return lax.all_to_all(values, "col", split_axis=0, concat_axis=1, tiled=True)


def token_layout(values):
    return lax.all_to_all(values, "col", split_axis=1, concat_axis=0, tiled=True)


def group_gather(values):
    return (
        lax.all_gather(values[0], ("row", "col"), axis=0, tiled=True),
        lax.all_gather(values[1], ("row", "col"), axis=0, tiled=True),
    )


def group_scatter(values):
    return lax.psum_scatter(
        values.astype(jnp.bfloat16), ("row", "col"), scatter_dimension=0, tiled=True
    ).astype(jnp.float32)


def rotate(values, positions, first_col, direction):
    row_total = values.shape[0]
    col_total = values.shape[1]
    pair_cols = first_col + 2 * jnp.arange(col_total // 2)
    pair_index = (pair_cols % HEAD_SIZE // 2).astype(jnp.float32)
    inverse = 1.0 / THETA ** (2.0 * pair_index / HEAD_SIZE)
    angles = positions.astype(jnp.float32)[:, None] * inverse[None, :]
    cosine = jnp.cos(angles)
    sine_part = jnp.sin(angles)
    pair_view = values.reshape(row_total, col_total // 2, 2)
    even_part = pair_view[:, :, 0]
    odd_part = pair_view[:, :, 1]
    turned = jnp.stack(
        [
            even_part * cosine - direction * odd_part * sine_part,
            direction * even_part * sine_part + odd_part * cosine,
        ],
        axis=2,
    )
    return turned.reshape(row_total, col_total)


def split_heads(values, kv_heads):
    row_total = values.shape[0]
    per_group = values.shape[1] // (kv_heads * HEAD_SIZE)
    shaped = values.reshape(row_total, kv_heads, per_group, HEAD_SIZE).transpose(1, 2, 0, 3)
    return shaped.reshape(kv_heads, per_group * row_total, HEAD_SIZE)


def heads_merge(values, row_total):
    kv_heads = values.shape[0]
    per_group = values.shape[1] // row_total
    shaped = values.reshape(kv_heads, per_group, row_total, values.shape[2]).transpose(2, 0, 1, 3)
    return shaped.reshape(row_total, kv_heads * per_group * values.shape[2])


def on_device(
    inputs,
    first_gain,
    query_weight,
    key_matrix,
    value_matrix,
    output_weight,
    second_gain,
    gate_weight,
    up_weight,
    down_weight,
    cotangent,
):
    col_count = lax.axis_size("col")
    source = inputs.astype(jnp.float32)
    first_scale, first_normed = norm_forward(source, first_gain)
    query_cols = query_weight.shape[1]
    key_cols = key_matrix.shape[1]
    joint_weight = jnp.concatenate([query_weight, key_matrix, value_matrix], axis=1)
    joint_rows, first_whole = rows_project(first_normed, joint_weight)
    row_tokens = joint_rows.shape[0]
    row_pos = (lax.axis_index("row") * row_tokens + jnp.arange(row_tokens)) % SEQUENCE_LENGTH
    col_index = lax.axis_index("col")
    query_rot = rotate(joint_rows[:, :query_cols], row_pos, col_index * query_cols, 1.0)
    key_rot = rotate(
        joint_rows[:, query_cols : query_cols + key_cols], row_pos, col_index * key_cols, 1.0
    )
    joint_low = jnp.concatenate(
        [query_rot, key_rot, joint_rows[:, query_cols + key_cols :]], axis=1
    ).astype(jnp.bfloat16)
    joint_heads = head_layout(joint_low)
    rows_of_query = joint_heads.shape[0]
    joint_heads = joint_heads.reshape(rows_of_query, col_count, query_cols + 2 * key_cols)
    every_query = joint_heads[:, :, :query_cols].reshape(rows_of_query, col_count * query_cols)
    key_local = joint_heads[:, :, query_cols : query_cols + key_cols].reshape(
        rows_of_query, col_count * key_cols
    )
    value_local = joint_heads[:, :, query_cols + key_cols :].reshape(
        rows_of_query, col_count * key_cols
    )
    key_all, value_all = group_gather((key_local, value_local))
    width_of_key = KEY_VALUE_HEADS * HEAD_SIZE
    query_groups = QUERY_HEADS // KEY_VALUE_HEADS
    keys_in_block = min(512, SEQUENCE_LENGTH)
    soft_scale = 1.0 / math.sqrt(HEAD_SIZE)
    device_block = lax.axis_index("row") * col_count + lax.axis_index("col")
    group_first = device_block * rows_of_query
    seq_first = group_first // SEQUENCE_LENGTH * SEQUENCE_LENGTH
    local_first = group_first - seq_first
    total_blocks = (local_first + rows_of_query - 1) // keys_in_block + 1
    query_pos = local_first + jnp.arange(query_groups * rows_of_query) % rows_of_query
    split_queries = split_heads(every_query, KEY_VALUE_HEADS)

    def block_scores(block_index):
        keys_block_slice = lax.dynamic_slice_in_dim(
            key_all, block_index * keys_in_block, keys_in_block, 0
        )
        keys_block_slice = keys_block_slice.reshape(
            keys_in_block, KEY_VALUE_HEADS, HEAD_SIZE
        ).transpose(1, 0, 2)
        values_block_slice = lax.dynamic_slice_in_dim(
            value_all, block_index * keys_in_block, keys_in_block, 0
        )
        values_block_slice = values_block_slice.reshape(
            keys_in_block, KEY_VALUE_HEADS, HEAD_SIZE
        ).transpose(1, 0, 2)
        raw_scores = jnp.einsum(
            "gqd,gkd->gqk", split_queries, keys_block_slice, preferred_element_type=jnp.float32
        )
        allowed = (block_index * keys_in_block + jnp.arange(keys_in_block))[
            None, None, :
        ] <= query_pos[None, :, None]
        return (raw_scores * soft_scale, allowed, keys_block_slice, values_block_slice)

    def max_step(block_index, carried):
        running_max, running_sum = carried
        scores, allowed, keys_block_slice, values_block_slice = block_scores(block_index)
        masked = jnp.where(allowed, scores, NEGATIVE_FILL)
        new_max = jnp.maximum(running_max, jnp.max(masked, axis=2))
        kept_terms = jnp.where(allowed, jnp.exp(masked - new_max[:, :, None]), 0.0)
        running_sum = running_sum * jnp.exp(running_max - new_max) + jnp.sum(kept_terms, axis=2)
        return (new_max, running_sum)

    initial_maximum = jnp.full(
        (KEY_VALUE_HEADS, query_groups * rows_of_query), NEGATIVE_FILL, jnp.float32
    )
    final_max, final_sum = lax.fori_loop(
        0, total_blocks, max_step, (initial_maximum, jnp.zeros_like(initial_maximum))
    )
    log_total = final_max + jnp.log(final_sum)

    def mixing_step(block_index, attended_acc):
        scores, allowed, keys_block_slice, values_block_slice = block_scores(block_index)
        prob_block = jnp.where(allowed, jnp.exp(scores - log_total[:, :, None]), 0.0).astype(
            jnp.bfloat16
        )
        return attended_acc + jnp.einsum(
            "gqk,gkd->gqd", prob_block, values_block_slice, preferred_element_type=jnp.float32
        )

    attended_split = lax.fori_loop(
        0,
        total_blocks,
        mixing_step,
        jnp.zeros((KEY_VALUE_HEADS, query_groups * rows_of_query, HEAD_SIZE), jnp.float32),
    )
    attended = heads_merge(attended_split, rows_of_query)
    attended_rows = token_layout(attended.astype(jnp.bfloat16))
    attn_out, attended_whole = cols_project(attended_rows, output_weight)
    middle = source + attn_out
    second_scale, second_normed = norm_forward(middle, second_gain)
    hidden_cols = gate_weight.shape[1]
    gate_up_weight = jnp.concatenate([gate_weight, up_weight], axis=1)
    gate_up, second_whole = rows_project(second_normed, gate_up_weight)
    gate_values = gate_up[:, :hidden_cols]
    up_values = gate_up[:, hidden_cols:]
    sigmoid_gate = jax.nn.sigmoid(gate_values)
    active = (gate_values * sigmoid_gate * up_values).astype(jnp.bfloat16)
    ffn_out, active_whole = cols_project(active, down_weight)
    d_active, upstream_whole = rows_project(cotangent, down_weight.T)
    down_grad = contract_rows(active_whole, upstream_whole)
    d_gate = (
        d_active * up_values * sigmoid_gate * (1.0 + gate_values * (1.0 - sigmoid_gate))
    ).astype(jnp.bfloat16)
    d_up = (d_active * gate_values * sigmoid_gate).astype(jnp.bfloat16)
    d_second, d_gate_up_whole = cols_project(
        jnp.concatenate([d_gate, d_up], axis=1), gate_up_weight.T
    )
    gate_up_grad = contract_rows(second_whole, d_gate_up_whole)
    gate_grad = gate_up_grad[:, :hidden_cols]
    up_grad = gate_up_grad[:, hidden_cols:]
    result = (middle + ffn_out).astype(jnp.bfloat16)
    upstream = cotangent.astype(jnp.float32)
    second_back, second_gain_grad = norm_backward(middle, second_scale, second_gain, d_second)
    d_middle = upstream + second_back
    d_attn = d_middle.astype(jnp.bfloat16)
    d_attended_rows, d_attn_whole = rows_project(d_attn, output_weight.T)
    output_grad = contract_rows(attended_whole, d_attn_whole)
    attended_gradient = head_layout(d_attended_rows.astype(jnp.bfloat16))
    attended_gradient_split = split_heads(attended_gradient, KEY_VALUE_HEADS)
    row_dots = jnp.sum(attended_gradient_split.astype(jnp.float32) * attended_split, axis=2)

    def grad_step(block_index, carried):
        query_acc, key_buffer = carried
        scores, allowed, keys_block_slice, values_block_slice = block_scores(block_index)
        prob_block = jnp.where(allowed, jnp.exp(scores - log_total[:, :, None]), 0.0)
        prob_low = prob_block.astype(jnp.bfloat16)
        d_probs = jnp.einsum(
            "gqd,gkd->gqk",
            attended_gradient_split,
            values_block_slice,
            preferred_element_type=jnp.float32,
        )
        d_raw = (prob_block * (d_probs - row_dots[:, :, None]) * soft_scale).astype(jnp.bfloat16)
        query_acc = query_acc + jnp.einsum(
            "gqk,gkd->gqd", d_raw, keys_block_slice, preferred_element_type=jnp.float32
        )
        key_part = jnp.einsum(
            "gqk,gqd->gkd", d_raw, split_queries, preferred_element_type=jnp.float32
        )
        value_part = jnp.einsum(
            "gqk,gqd->gkd", prob_low, attended_gradient_split, preferred_element_type=jnp.float32
        )
        block_grads = jnp.concatenate(
            [
                key_part.transpose(1, 0, 2).reshape(keys_in_block, width_of_key),
                value_part.transpose(1, 0, 2).reshape(keys_in_block, width_of_key),
            ],
            axis=1,
        )
        key_buffer = lax.dynamic_update_slice_in_dim(
            key_buffer, block_grads, block_index * keys_in_block, 0
        )
        return (query_acc, key_buffer)

    start_grads = (
        jnp.zeros_like(attended_split),
        jnp.zeros((SEQUENCE_LENGTH, 2 * width_of_key), jnp.float32),
    )
    query_acc, key_buffer = lax.fori_loop(0, total_blocks, grad_step, start_grads)
    key_grads = group_scatter(key_buffer)
    local_pos = local_first + jnp.arange(rows_of_query)
    d_query = rotate(heads_merge(query_acc, rows_of_query), local_pos, 0, -1.0).astype(jnp.bfloat16)
    d_key = rotate(key_grads[:, :width_of_key], local_pos, 0, -1.0).astype(jnp.bfloat16)
    d_value = key_grads[:, width_of_key:].astype(jnp.bfloat16)
    packed = jnp.concatenate(
        [
            d_query.reshape(rows_of_query, col_count, query_cols),
            d_key.reshape(rows_of_query, col_count, key_cols),
            d_value.reshape(rows_of_query, col_count, key_cols),
        ],
        axis=2,
    )
    d_joint_rows = token_layout(
        packed.reshape(rows_of_query, col_count * (query_cols + 2 * key_cols))
    )
    d_first, d_joint_whole = cols_project(d_joint_rows, joint_weight.T)
    joint_grad = contract_rows(first_whole, d_joint_whole)
    first_back, first_gain_grad = norm_backward(source, first_scale, first_gain, d_first)
    input_grad = (d_middle + first_back).astype(jnp.bfloat16)
    weight_sums = (
        lax.psum(joint_grad.astype(jnp.bfloat16), "dp").astype(jnp.float32),
        lax.psum(output_grad.astype(jnp.bfloat16), "dp").astype(jnp.float32),
        lax.psum(gate_grad.astype(jnp.bfloat16), "dp").astype(jnp.float32),
        lax.psum(up_grad.astype(jnp.bfloat16), "dp").astype(jnp.float32),
        lax.psum(down_grad.astype(jnp.bfloat16), "dp").astype(jnp.float32),
    )
    gain_sums = lax.psum((first_gain_grad, second_gain_grad), ("dp", "col"))
    joint_sum = weight_sums[0]
    return (
        result,
        input_grad,
        gain_sums[0],
        joint_sum[:, :query_cols],
        joint_sum[:, query_cols : query_cols + key_cols],
        joint_sum[:, query_cols + key_cols :],
        weight_sums[1],
        gain_sums[1],
        weight_sums[2],
        weight_sums[3],
        weight_sums[4],
    )


def solution(mesh):
    placed = (
        P(("dp", "col"), "row"),
        P("row"),
        P("row", "col"),
        P("row", "col"),
        P("row", "col"),
        P("col", "row"),
        P("row"),
        P("row", "col"),
        P("row", "col"),
        P("col", "row"),
        P(("dp", "col"), "row"),
    )
    return jax.shard_map(
        on_device,
        mesh=mesh,
        in_specs=placed,
        out_specs=(
            P(("dp", "col"), "row"),
            P(("dp", "col"), "row"),
            P("row"),
            P("row", "col"),
            P("row", "col"),
            P("row", "col"),
            P("col", "row"),
            P("row"),
            P("row", "col"),
            P("row", "col"),
            P("col", "row"),
        ),
        check_vma=False,
    )
```

profile of v0, /device:TPU:0, one launch (start us, length us, event | category | flops | bytes accessed | tf_op | source)
XLA Modules:
  0.0 618.5 jit_solution(69171348134949971)
XLA Ops:
  8.2 8.4 %psum.77 = f32[512]{0:T(512)S(1)} all-reduce(f32[512]{0:T(512)S(1)} %fusion.50), channel_id=1, replica_groups=mesh['dp'=2,'row'=4,'col'=4] {'row'}, use_global_device_ids=true, to_apply=%region_1.0 | all-reduce | flops 512 | bytes 4096 | tf_op jit(solution)/shard_map/psum | solution.py:20
  18.2 15.8 %all_gather.30 = bf16[2048,144]{0,1:T(8,128)(2,1)S(1)} all-gather(bf16[512,144]{0,1:T(8,128)(2,1)S(1)} %fusion.52), channel_id=1, replica_groups=mesh['dp'=2,'row'=4,'col'=4] {'col'}, dimensions={0}, use_global_device_ids=true | all-gather | bytes 737280 | tf_op jit(solution)/shard_map/all_gather | solution.py:47
  38.3 25.7 %reduce-scatter.12.cloned.1.call-done = bf16[512,240]{0,1:T(8,128)(2,1)} async-done(((bf16[2048,240]{0,1:T(8,128)(2,1)}), bf16[512,240]{0,1:T(8,128)(2,1)}) %reduce-scatter.12.cloned.1.call-update) | async-done | bytes 245776 | tf_op jit(solution)/shard_map/reduce_scatter | solution.py:49
  67.8 4.6 all-to-all-start
  72.4 8.4 %all-to-all-done = bf16[4,128,240]{1,2,0:T(8,128)(2,1)S(1)} async-done(((bf16[4,128,240]{1,2,0:T(8,128)(2,1)}), bf16[4,128,240]{1,2,0:T(8,128)(2,1)S(1)}, u32[]{:S(2)}, u32[]{:S(2)}) %all-to-all-start) | async-done | bytes 245792 | tf_op jit(solution)/shard_map/all_to_all | solution.py:73
  80.8 38.2 %all_gather.31 = bf16[2048,192]{0,1:T(8,128)(2,1)S(1)} all-gather(bf16[128,192]{0,1:T(8,128)(2,1)S(1)} %bitcast.227), channel_id=1, replica_groups=mesh['dp'=2,'row'=4,'col'=4] {'row','col'}, dimensions={0}, use_global_device_ids=true | all-gather | bytes 835584 | tf_op jit(solution)/shard_map/all_gather | solution.py:82
  120.6 39.4 %all_gather.32 = bf16[2048,192]{0,1:T(8,128)(2,1)S(1)} all-gather(bf16[128,192]{0,1:T(8,128)(2,1)S(1)} %bitcast.226), channel_id=1, replica_groups=mesh['dp'=2,'row'=4,'col'=4] {'row','col'}, dimensions={0}, use_global_device_ids=true | all-gather | bytes 835584 | tf_op jit(solution)/shard_map/all_gather | solution.py:83
  162.6 9.5 %all_to_all.61 = bf16[128,4,144]{0,2,1:T(8,128)(2,1)S(1)} all-to-all(bf16[128,4,144]{0,2,1:T(8,128)(2,1)S(1)} %bitcast.222), channel_id=1, replica_groups=mesh['dp'=2,'row'=4,'col'=4] {'col'}, dimensions={1} | all-to-all | bytes 294912 | tf_op jit(solution)/shard_map/all_to_all | solution.py:77
  172.2 11.2 %all_gather.33 = bf16[2048,144]{0,1:T(8,128)(2,1)S(1)} all-gather(bf16[512,144]{0,1:T(8,128)(2,1)S(1)} %copy_bitcast_fusion.2), channel_id=1, replica_groups=mesh['dp'=2,'row'=4,'col'=4] {'row'}, dimensions={0}, use_global_device_ids=true | all-gather | bytes 737280 | tf_op jit(solution)/shard_map/all_gather | solution.py:60
  185.6 21.9 %reduce-scatter.14.cloned.1.call-done = bf16[512,144]{0,1:T(8,128)(2,1)} async-done(((bf16[2048,144]{0,1:T(8,128)(2,1)}), bf16[512,144]{0,1:T(8,128)(2,1)}) %reduce-scatter.14.cloned.1.call-update) | async-done | bytes 147472 | tf_op jit(solution)/shard_map/reduce_scatter | solution.py:62
  208.5 5.7 psum.78
  215.7 16.6 %all_gather.34 = bf16[2048,144]{0,1:T(8,128)(2,1)S(1)} all-gather(bf16[512,144]{0,1:T(8,128)(2,1)S(1)} %multiply_convert_fusion.1), channel_id=1, replica_groups=mesh['dp'=2,'row'=4,'col'=4] {'col'}, dimensions={0}, use_global_device_ids=true | all-gather | bytes 737280 | tf_op jit(solution)/shard_map/all_gather | solution.py:47
  236.8 15.8 %all_gather.36 = bf16[2048,144]{0,1:T(8,128)(2,1)S(1)} all-gather(bf16[512,144]{0,1:T(8,128)(2,1)S(1)} %copy-done.20), channel_id=1, replica_groups=mesh['dp'=2,'row'=4,'col'=4] {'col'}, dimensions={0}, use_global_device_ids=true | all-gather | bytes 737280 | tf_op jit(solution)/shard_map/all_gather | solution.py:47
  255.4 16.9 %reduce-scatter.16.cloned.1.call-done = bf16[512,768]{1,0:T(8,128)(2,1)} async-done(((bf16[2048,768]{1,0:T(8,128)(2,1)}), bf16[512,768]{1,0:T(8,128)(2,1)}) %reduce-scatter.16.cloned.1.call-update) | async-done | bytes 786448 | tf_op jit(solution)/shard_map/reduce_scatter | solution.py:49
  273.5 29.2 %reduce-scatter.20.cloned.1.call-done = bf16[512,384]{1,0:T(8,128)(2,1)} async-done(((bf16[2048,384]{1,0:T(8,128)(2,1)}), bf16[512,384]{1,0:T(8,128)(2,1)}) %reduce-scatter.20.cloned.1.call-update) | async-done | bytes 393232 | tf_op jit(solution)/shard_map/reduce_scatter | solution.py:49
  306.0 28.6 %all-gather.5.cloned.1.call-done = bf16[2048,768]{1,0:T(8,128)(2,1)} async-done(((bf16[512,768]{1,0:T(8,128)(2,1)}), bf16[2048,768]{1,0:T(8,128)(2,1)}) %all-gather.5.cloned.1.call-update) | async-done | bytes 3145744 | tf_op jit(solution)/shard_map/all_gather | solution.py:60
  338.5 22.3 %reduce-scatter.22.cloned.1.call-done = bf16[512,144]{0,1:T(8,128)(2,1)} async-done(((bf16[2048,144]{0,1:T(8,128)(2,1)}), bf16[512,144]{0,1:T(8,128)(2,1)}) %reduce-scatter.22.cloned.1.call-update) | async-done | bytes 147472 | tf_op jit(solution)/shard_map/reduce_scatter | solution.py:62
  362.4 5.6 psum.79
  369.1 16.8 %all_gather.38 = bf16[2048,144]{0,1:T(8,128)(2,1)S(1)} all-gather(bf16[512,144]{0,1:T(8,128)(2,1)S(1)} %fusion.90), channel_id=1, replica_groups=mesh['dp'=2,'row'=4,'col'=4] {'col'}, dimensions={0}, use_global_device_ids=true | all-gather | bytes 737280 | tf_op jit(solution)/shard_map/all_gather | solution.py:47
  387.9 20.7 %reduce-scatter.24.cloned.1.call-done = bf16[512,144]{0,1:T(8,128)(2,1)} async-done(((bf16[2048,144]{0,1:T(8,128)(2,1)}), bf16[512,144]{0,1:T(8,128)(2,1)}) %reduce-scatter.24.cloned.1.call-update) | async-done | bytes 147472 | tf_op jit(solution)/shard_map/reduce_scatter | solution.py:49
  410.2 4.6 all-to-all-start.2
  415.6 5.5 all-to-all-done.2
  422.6 5.6 while.39
  432.5 4.8 all-gather.3.cloned.1.call-done
  443.7 60.4 %reduce-scatter.28.cloned.1.call-done = bf16[128,384]{1,0:T(8,128)(2,1)} async-done(((bf16[2048,384]{1,0:T(8,128)(2,1)}), bf16[128,384]{1,0:T(8,128)(2,1)}) %reduce-scatter.28.cloned.1.call-update) | async-done | bytes 98320
  516.0 4.2 all-to-all-done.3
  520.2 9.2 %all_gather.39 = bf16[2048,240]{0,1:T(8,128)(2,1)S(1)} all-gather(bf16[512,240]{0,1:T(8,128)(2,1)S(1)} %copy_bitcast_fusion), channel_id=1, replica_groups=mesh['dp'=2,'row'=4,'col'=4] {'row'}, dimensions={0}, use_global_device_ids=true | all-gather | bytes 1228800 | tf_op jit(solution)/shard_map/all_gather | solution.py:60
  536.0 9.8 %psum.83 = bf16[144,144]{1,0:T(8,128)(2,1)S(1)} all-reduce(bf16[144,144]{1,0:T(8,128)(2,1)S(1)} %convolution_convert_fusion.10), channel_id=1, replica_groups=mesh['dp'=2,'row'=4,'col'=4] {'dp'}, use_global_device_ids=true, to_apply=%region_29.30 | all-reduce | flops 20736 | bytes 82944 | tf_op jit(solution)/shard_map/psum | solution.py:331
  546.5 12.3 %all-reduce.4.cloned.1.call-done = (bf16[144,240]{1,0:T(8,128)(2,1)}, bf16[144,384]{1,0:T(8,128)(2,1)}, bf16[144,384]{1,0:T(8,128)(2,1)}, bf16[384,144]{0,1:T(8,128)(2,1)}) async-done(((bf16[144,240]{1,0:T(8,128)(2,1)}, bf16[144,384]{1,0:T(8,128)(2,1)}, bf16[144,384]{1,0:T(8,128)(2,1)}, bf16[384,144]{0,1:T(8,128)(2,1)}), (bf16[144,240]{1,0:T(8,128)(2,1)}, bf16[144,384]{1,0:T(8,128)(2,1)}, ...) | async-done | bytes 400912 | tf_op jit(solution)/shard_map/psum | solution.py:330
  567.4 16.0 %reduce-scatter.26.cloned.1.call-done = bf16[512,144]{0,1:T(8,128)(2,1)} async-done(((bf16[2048,144]{0,1:T(8,128)(2,1)}), bf16[512,144]{0,1:T(8,128)(2,1)}) %reduce-scatter.26.cloned.1.call-update) | async-done | bytes 147472 | tf_op jit(solution)/shard_map/reduce_scatter | solution.py:62
  584.5 19.4 %all-reduce = (f32[144]{0:T(256)}, f32[144]{0:T(256)}) all-reduce(f32[144]{0:T(256)S(1)} %get-tuple-element.327, f32[144]{0:T(256)S(1)} %copy-done.42), channel_id=1, replica_groups=mesh['dp'=2,'row'=4,'col'=4] {'dp','col'}, use_global_device_ids=true, to_apply=%region_27.28 | all-reduce | flops 288 | bytes 2304 | tf_op jit(solution)/shard_map/psum | solution.py:336
  603.9 5.6 psum.80
  (233 shorter events, 93.6 us)
Async XLA Ops:
  7.2 246.2 %copy-start = (bf16[384,144]{0,1:T(8,128)(2,1)S(1)}, bf16[384,144]{0,1:T(8,128)(2,1)}, u32[]{:S(2)}) copy-start(bf16[384,144]{0,1:T(8,128)(2,1)} %param.26) | copy-start | bytes 331780
  7.2 56.8 %reduce-scatter.12.cloned.1.call-start = ((), (), s32[]{:S(2)}) async-start(), calls=%async_computation.13 | async-start | bytes 1228800 | tf_op jit(solution)/shard_map/reduce_scatter | solution.py:49
  67.8 12.9 %all-to-all-start = ((bf16[4,128,240]{1,2,0:T(8,128)(2,1)}), bf16[4,128,240]{1,2,0:T(8,128)(2,1)S(1)}, u32[]{:S(2)}, u32[]{:S(2)}) async-start(bf16[4,128,240]{1,2,0:T(8,128)(2,1)} %copy.153), calls=%async_computation.1 | async-start | bytes 491520 | tf_op jit(solution)/shard_map/all_to_all | solution.py:73
  72.4 135.1 %reduce-scatter.14.cloned.1.call-start = ((), (), s32[]{:S(2)}) async-start(), calls=%async_computation.14 | async-start | bytes 737280 | tf_op jit(solution)/shard_map/reduce_scatter | solution.py:62
  162.6 52.2 %copy-start.37 = (f32[144]{0:T(256)S(1)}, f32[144]{0:T(256)}, u32[]{:S(2)}) copy-start(f32[144]{0:T(256)} %param.23) | copy-start | bytes 1732
  185.4 86.8 %reduce-scatter.16.cloned.1.call-start = ((), (), s32[]{:S(2)}) async-start(), calls=%async_computation.15 | async-start | bytes 3932160 | tf_op jit(solution)/shard_map/reduce_scatter | solution.py:49
  185.5 50.3 %copy-start.17 = (bf16[144,768]{1,0:T(8,128)(2,1)}, bf16[144,768]{1,0:T(8,128)(2,1)S(1)}, u32[]{:S(2)}) copy-start(bf16[144,768]{1,0:T(8,128)(2,1)S(1)} %constant_dynamic-update-slice_fusion) | copy-start | bytes 663556
  235.9 66.8 %reduce-scatter.20.cloned.1.call-start = ((), (), s32[]{:S(2)}) async-start(), calls=%async_computation.18 | async-start | bytes 1966080 | tf_op jit(solution)/shard_map/reduce_scatter | solution.py:49
  255.3 79.2 %all-gather.5.cloned.1.call-start = ((), (), s32[]{:S(2)}) async-start(), calls=%async_computation.19 | async-start | bytes 3932160 | tf_op jit(solution)/shard_map/all_gather | solution.py:60
  305.9 54.9 %copy-start.13 = (bf16[512,144]{0,1:T(8,128)(2,1)S(1)}, bf16[512,144]{0,1:T(8,128)(2,1)}, u32[]{:S(2)}) copy-start(bf16[512,144]{0,1:T(8,128)(2,1)} %reduce-scatter.14.cloned.1.call-done) | copy-start | bytes 442372
  305.9 54.9 %copy-start.38 = (f32[144]{0:T(256)S(1)}, f32[144]{0:T(256)}, u32[]{:S(2)}) copy-start(f32[144]{0:T(256)} %param.23) | copy-start | bytes 1732
  305.9 62.1 %copy-start.21 = (bf16[512,144]{0,1:T(8,128)(2,1)S(1)}, bf16[512,144]{0,1:T(8,128)(2,1)}, u32[]{:S(2)}) copy-start(bf16[512,144]{0,1:T(8,128)(2,1)} %param.27) | copy-start | bytes 442372
  305.9 62.1 %copy-start.33 = (f32[512]{0:T(512)S(1)}, f32[512]{0:T(512)}, u32[]{:S(2)}) copy-start(f32[512]{0:T(512)} %get-tuple-element.424) | copy-start | bytes 6148
  305.9 54.9 %reduce-scatter.22.cloned.1.call-start = ((), (), s32[]{:S(2)}) async-start(), calls=%async_computation.20 | async-start | bytes 737280 | tf_op jit(solution)/shard_map/reduce_scatter | solution.py:62
  338.5 82.6 %copy-start.16 = (f32[3,384,64]{1,2,0:T(8,128)S(1)}, f32[3,384,64]{1,2,0:T(8,128)}, u32[]{:S(2)}) copy-start(f32[3,384,64]{1,2,0:T(8,128)} %copy-done.15) | copy-start | bytes 884740
  338.5 70.2 %reduce-scatter.24.cloned.1.call-start = ((), (), s32[]{:S(2)}) async-start(), calls=%async_computation.21 | async-start | bytes 737280 | tf_op jit(solution)/shard_map/reduce_scatter | solution.py:49
  368.1 53.1 %copy-start.35 = (f32[512]{0:T(512)}, f32[512]{0:T(512)S(1)}, u32[]{:S(2)}) copy-start(f32[512]{0:T(512)S(1)} %psum.79) | copy-start | bytes 6148
  410.2 10.8 %all-to-all-start.2 = ((bf16[4,128,144]{1,2,0:T(8,128)(2,1)}), bf16[4,128,144]{1,2,0:T(8,128)(2,1)S(1)}, u32[]{:S(2)}, u32[]{:S(2)}) async-start(bf16[4,128,144]{1,2,0:T(8,128)(2,1)} %copy_bitcast_fusion.4), calls=%async_computation.9 | async-start | bytes 294912 | tf_op jit(solution)/shard_map/all_to_all | solution.py:73
  414.8 22.5 %all-gather.3.cloned.1.call-start = ((), (), s32[]{:S(2)}) async-start(), calls=%async_computation.16 | async-start | bytes 1966080 | tf_op jit(solution)/shard_map/all_gather | solution.py:60
  415.6 88.6 %reduce-scatter.28.cloned.1.call-start = ((), (), s32[]{:S(2)}) async-start(), calls=%async_computation.23 | async-start | bytes 1671168
  439.9 73.6 %copy-start.1 = (bf16[2048,768]{1,0:T(8,128)(2,1)S(1)}, bf16[2048,768]{1,0:T(8,128)(2,1)}, u32[]{:S(2)}) copy-start(bf16[2048,768]{1,0:T(8,128)(2,1)} %all-gather.5.cloned.1.call-done) | copy-start | bytes 9437188
  510.0 10.2 %all-to-all-start.3 = ((bf16[128,4,240]{0,2,1:T(8,128)(2,1)}), bf16[128,4,240]{0,2,1:T(8,128)(2,1)S(1)}, u32[]{:S(2)}, u32[]{:S(2)}) async-start(bf16[128,4,240]{0,2,1:T(8,128)(2,1)} %pad_maximum_fusion.2), calls=%async_computation.10 | async-start | bytes 491520 | tf_op jit(solution)/shard_map/all_to_all | solution.py:77
  513.5 45.2 %all-reduce.4.cloned.1.call-start = ((), (), s32[]{:S(2)}) async-start(), calls=%async_computation.24 | async-start | bytes 811008 | tf_op jit(solution)/shard_map/psum | solution.py:330
  531.7 51.7 %reduce-scatter.26.cloned.1.call-start = ((), (), s32[]{:S(2)}) async-start(), calls=%async_computation.22 | async-start | bytes 737280 | tf_op jit(solution)/shard_map/reduce_scatter | solution.py:62
  534.0 75.6 %reduce-scatter.18.cloned.1.call-start = ((), (), s32[]{:S(2)}) async-start(), calls=%async_computation.17 | async-start | bytes 737280 | tf_op jit(solution)/shard_map/reduce_scatter | solution.py:62
  535.5 74.0 %copy-start.14 = (bf16[512,144]{0,1:T(8,128)(2,1)S(1)}, bf16[512,144]{0,1:T(8,128)(2,1)}, u32[]{:S(2)}) copy-start(bf16[512,144]{0,1:T(8,128)(2,1)} %reduce-scatter.14.cloned.1.call-done) | copy-start | bytes 442372
  535.5 74.0 %copy-start.19 = (bf16[512,144]{0,1:T(8,128)(2,1)S(1)}, bf16[512,144]{0,1:T(8,128)(2,1)}, u32[]{:S(2)}) copy-start(bf16[512,144]{0,1:T(8,128)(2,1)} %reduce-scatter.22.cloned.1.call-done) | copy-start | bytes 442372
  535.5 74.0 %copy-start.22 = (bf16[512,144]{0,1:T(8,128)(2,1)S(1)}, bf16[512,144]{0,1:T(8,128)(2,1)}, u32[]{:S(2)}) copy-start(bf16[512,144]{0,1:T(8,128)(2,1)} %param.27) | copy-start | bytes 442372
  535.6 74.0 %copy-start.34 = (f32[512]{0:T(512)S(1)}, f32[512]{0:T(512)}, u32[]{:S(2)}) copy-start(f32[512]{0:T(512)} %get-tuple-element.424) | copy-start | bytes 6148
  535.6 74.0 %copy-start.36 = (f32[512]{0:T(512)S(1)}, f32[512]{0:T(512)}, u32[]{:S(2)}) copy-start(f32[512]{0:T(512)} %copy-done.35) | copy-start | bytes 6148
  535.6 74.0 %copy-start.39 = (f32[144]{0:T(256)S(1)}, f32[144]{0:T(256)}, u32[]{:S(2)}) copy-start(f32[144]{0:T(256)} %param.23) | copy-start | bytes 1732
  535.6 74.0 %copy-start.41 = (f32[512]{0:T(512)S(1)}, f32[512]{0:T(512)}, u32[]{:S(2)}) copy-start(f32[512]{0:T(512)} %get-tuple-element.422) | copy-start | bytes 6148
  (27 other events, 557.2 us)
Sparse Core Ops, SparseCore 0:
  38.3 25.6 reduce-scatter.11
  185.5 21.8 reduce-scatter.13
  236.0 36.1 reduce-scatter.15
  274.6 28.0 reduce-scatter.19
  306.0 28.4 all-gather.4
  338.6 22.1 reduce-scatter.21
  388.1 20.5 reduce-scatter.23
  417.2 20.1 all-gather.2
  441.0 63.0 reduce-scatter.27
  531.8 26.8 all-reduce.3
  561.1 22.3 reduce-scatter.25
  585.6 20.5 reduce-scatter.17
where the time goes:
time: 621 us; the launch traced here: 618 us
  waiting for transfers between devices  278 us (45%)
  blocking collectives  227 us (37%)
  matrix products  30.3 us (5%)
  other arithmetic  30.1 us (5%)
  local copies, waits for them, and re-layouts  25 us (4%)
  between operations  15 us (2%)
  starting transfers between devices  13.1 us (2%)
    reduce_scatter x4, waiting for transfers between devices, rows_project(): lax.psum_scatter(jnp.dot(gathered, weight, preferred_element_type=jnp.flo...  92.5 us
    all_gather x4, blocking collectives, rows_project(): gathered = lax.all_gather(values, 'col', axis=0, tiled=True)  65 us
    unnamed x13, waiting for transfers between devices  61.3 us
    reduce_scatter x4, waiting for transfers between devices, cols_project(): lax.psum_scatter(jnp.dot(gathered, weight, preferred_element_type=jnp.flo...  60.2 us
    all_gather x1, blocking collectives, group_gather(): lax.all_gather(values[1], ('row', 'col'), axis=0, tiled=True)  39.4 us
    all_gather x1, blocking collectives, group_gather(): lax.all_gather(values[0], ('row', 'col'), axis=0, tiled=True)  38.2 us
    all_gather x2, waiting for transfers between devices, cols_project(): gathered = lax.all_gather(values, 'row', axis=0, tiled=True)  33.4 us
    psum x4, blocking collectives, feature_sums(): return lax.psum(values, 'row')  25.3 us
  transfers between devices with their start and end apart: 15, of which 14 were waited for; matrix products, arithmetic and copies ran while one was open for 6% of the time, Pallas kernels for 0%

commit v1 on v0

v1 whole, which is shorter than its diff:
```python
import functools
import math

import jax
import jax.numpy as jnp
from jax import lax
from jax.experimental import pallas as pl
from jax.experimental.pallas import tpu as pltpu
from jax.sharding import PartitionSpec as P

QUERY_HEADS = 9
KEY_VALUE_HEADS = 3
HEAD_SIZE = 64
SEQUENCE_LENGTH = 2048
EPS = 1e-05
THETA = 100000.0
NEGATIVE_FILL = -1e30
MESH = pl.DeviceIdType.MESH
BF = jnp.bfloat16
F32 = jnp.float32


def exchange_kernel(plan, axes, *refs):
    count = len(plan)
    ins, outs = refs[:count], refs[count : 2 * count]
    send_sem, recv_sem, local_sem = refs[2 * count :]
    barrier = pltpu.get_barrier_semaphore()
    total = 0
    for axis, size in axes:
        me = lax.axis_index(axis)
        for step in range(1, size):
            pl.semaphore_signal(
                barrier, inc=1, device_id={axis: lax.rem(me + step, size)}, device_id_type=MESH
            )
        total += size - 1
    pl.semaphore_wait(barrier, total)
    sizes = dict(axes)
    copies = []
    for item, (axis, mode) in enumerate(plan):
        size = sizes[axis]
        me = lax.axis_index(axis)
        for step in range(1, size):
            peer = lax.rem(me + step, size)
            source = ins[item] if mode == "g" else ins[item].at[peer]
            copy = pltpu.make_async_remote_copy(
                src_ref=source,
                dst_ref=outs[item].at[me],
                send_sem=send_sem.at[item, step],
                recv_sem=recv_sem.at[item, step],
                device_id={axis: peer},
                device_id_type=MESH,
            )
            copy.start()
            copies.append(copy)
    for item, (axis, mode) in enumerate(plan):
        me = lax.axis_index(axis)
        source = ins[item] if mode == "g" else ins[item].at[me]
        copy = pltpu.make_async_copy(source, outs[item].at[me], local_sem.at[item])
        copy.start()
        copies.append(copy)
    for copy in copies:
        copy.wait()


def exchange(ident, *items):
    plan = tuple((axis, mode) for _, axis, mode in items)
    axes = tuple((axis, lax.axis_size(axis)) for axis in dict.fromkeys(a for a, _ in plan))
    arrays = [array for array, _, _ in items]
    widest = max(size for _, size in axes)
    out_shape = tuple(
        jax.ShapeDtypeStruct(
            ((lax.axis_size(axis),) + array.shape) if mode == "g" else array.shape, array.dtype
        )
        for array, axis, mode in items
    )
    spec = pl.BlockSpec(memory_space=pltpu.VMEM)
    return pl.pallas_call(
        functools.partial(exchange_kernel, plan, axes),
        out_shape=out_shape,
        in_specs=[spec] * len(arrays),
        out_specs=tuple([spec] * len(arrays)),
        scratch_shapes=[
            pltpu.SemaphoreType.DMA((len(arrays), widest)),
            pltpu.SemaphoreType.DMA((len(arrays), widest)),
            pltpu.SemaphoreType.DMA((len(arrays),)),
        ],
        compiler_params=pltpu.CompilerParams(
            collective_id=ident, has_side_effects=True
        ),
        name="exchange_%d" % ident,
    )(*arrays)


def dot(left, right, left_dim=1, right_dim=0):
    return lax.dot_general(
        left, right, (((left_dim,), (right_dim,)), ((), ())), preferred_element_type=F32
    )


def rotate(values, cosine, sine):
    repeats = values.shape[1] // HEAD_SIZE
    cosine = jnp.tile(cosine, (1, repeats))
    sine = jnp.tile(sine, (1, repeats))
    even = (jnp.arange(values.shape[1]) % 2 == 0)[None, :]
    partner = jnp.where(even, -jnp.roll(values, -1, axis=1), jnp.roll(values, 1, axis=1))
    return values * cosine + partner * sine


def group_split(values):
    rows = values.shape[0]
    per = values.shape[1] // (KEY_VALUE_HEADS * HEAD_SIZE)
    shaped = values.reshape(rows, KEY_VALUE_HEADS, per, HEAD_SIZE).transpose(1, 2, 0, 3)
    return shaped.reshape(KEY_VALUE_HEADS, per * rows, HEAD_SIZE)


def group_merge(values, rows):
    per = values.shape[1] // rows
    shaped = values.reshape(KEY_VALUE_HEADS, per, rows, HEAD_SIZE).transpose(2, 0, 1, 3)
    return shaped.reshape(rows, KEY_VALUE_HEADS * per * HEAD_SIZE)


def norm_scale(source):
    return lax.rsqrt(jnp.mean(source * source, axis=1, keepdims=True) + EPS)


def norm_back(source, scale, gain, upstream):
    inner = jnp.sum(upstream * gain * source, axis=1, keepdims=True)
    cubed = scale * scale * scale
    d_source = scale * gain * upstream - source * cubed * inner / source.shape[1]
    return d_source, jnp.sum(upstream * source * scale, axis=0)


def on_device(
    inputs,
    first_gain,
    query_weight,
    key_matrix,
    value_matrix,
    output_weight,
    second_gain,
    gate_weight,
    up_weight,
    down_weight,
    cotangent,
):
    rows = lax.axis_size("row")
    cols = lax.axis_size("col")
    block_tokens, feat = inputs.shape
    tokens = block_tokens // rows
    width = feat * rows
    hidden = gate_weight.shape[1]
    q_cols = query_weight.shape[1]
    k_cols = key_matrix.shape[1]
    row_index = lax.axis_index("row")
    col_index = lax.axis_index("col")
    soft_scale = 1.0 / math.sqrt(HEAD_SIZE)

    ffn_block = jnp.concatenate([gate_weight, up_weight, down_weight.T], axis=1)
    qo_block = jnp.concatenate([query_weight, key_matrix, value_matrix, output_weight.T], axis=1)
    joint = jnp.concatenate([inputs, cotangent], axis=1).reshape(rows, tokens, 2 * feat)
    gains = jnp.stack([first_gain, second_gain])
    joint_all, gain_all, ffn_all, qo_cols = exchange(
        0,
        (joint, "row", "s"),
        (gains, "row", "g"),
        (ffn_block, "row", "g"),
        (qo_block, "col", "g"),
    )
    joint_all = joint_all.transpose(1, 0, 2)
    source = joint_all[:, :, :feat].reshape(tokens, width).astype(F32)
    cot_low = joint_all[:, :, feat:].reshape(tokens, width)
    upstream = cot_low.astype(F32)
    gain_all = gain_all.transpose(1, 0, 2).reshape(2, width)
    gain1, gain2 = gain_all[0:1], gain_all[1:2]
    first_scale = norm_scale(source)
    normed1 = (source * first_scale * gain1).astype(BF)

    qo_all, cot_all = exchange(1, (qo_cols, "row", "g"), (cot_low, "col", "g"))
    qo_all = qo_all.transpose(0, 2, 1, 3).reshape(width, cols, q_cols * 2 + 2 * k_cols)
    at = 0
    parts = []
    for size in (q_cols, k_cols, k_cols, q_cols):
        parts.append(qo_all[:, :, at : at + size].reshape(width, cols * size))
        at += size
    qkv_weight = jnp.concatenate(parts[:3], axis=1)
    out_t = parts[3]
    kv_width = cols * k_cols

    first_pos = (col_index * block_tokens + row_index * tokens) % SEQUENCE_LENGTH
    positions = (first_pos + jnp.arange(tokens)).astype(F32)
    pair_index = (jnp.arange(HEAD_SIZE) // 2).astype(F32)
    inverse = 1.0 / THETA ** (2.0 * pair_index / HEAD_SIZE)
    angles = positions[:, None] * inverse[None, :]
    cosine, sine = jnp.cos(angles), jnp.sin(angles)

    qkv = dot(normed1, qkv_weight)
    turned = rotate(qkv[:, : width + kv_width], cosine, sine)
    queries = turned[:, :width].astype(BF)
    kv_low = jnp.concatenate([turned[:, width:], qkv[:, width + kv_width :]], axis=1).astype(BF)
    (kv_cols,) = exchange(2, (kv_low, "col", "g"))
    (kv_all,) = exchange(3, (kv_cols, "row", "g"))
    kv_all = kv_all.reshape(rows * cols * tokens, 2, KEY_VALUE_HEADS, HEAD_SIZE)
    keys = kv_all[:, 0].transpose(1, 0, 2)
    values = kv_all[:, 1].transpose(1, 0, 2)
    key_index = jnp.arange(rows * cols * tokens)
    key_row = key_index // (cols * tokens)
    key_col = key_index // tokens % cols
    key_global = key_col * block_tokens + key_row * tokens + key_index % tokens
    query_global = col_index * block_tokens + row_index * tokens + jnp.arange(tokens)
    query_global = jnp.tile(query_global, QUERY_HEADS // KEY_VALUE_HEADS)
    allowed = (key_global[None, :] <= query_global[:, None]) & (
        key_global[None, :] // SEQUENCE_LENGTH == query_global[:, None] // SEQUENCE_LENGTH
    )
    split_q = group_split(queries)
    scores = jnp.einsum("gqd,gkd->gqk", split_q, keys, preferred_element_type=F32) * soft_scale
    masked = jnp.where(allowed[None], scores, NEGATIVE_FILL)
    top = jnp.max(masked, axis=2, keepdims=True)
    terms = jnp.exp(masked - top)
    total = jnp.sum(terms, axis=2, keepdims=True)
    probs = terms / total
    probs_low = probs.astype(BF)
    att_split = jnp.einsum("gqk,gkd->gqd", probs_low, values, preferred_element_type=F32)
    attended = group_merge(att_split, tokens).astype(BF)
    middle = source + dot(attended, out_t, 1, 1)
    second_scale = norm_scale(middle)
    normed2 = (middle * second_scale * gain2).astype(BF)

    (normed2_all,) = exchange(4, (normed2, "col", "g"))
    normed2_all = normed2_all.reshape(cols * tokens, width)
    cot_all = cot_all.reshape(cols * tokens, width)
    ffn_all = ffn_all.reshape(width, 3 * hidden)
    gate_up = dot(normed2_all, ffn_all[:, : 2 * hidden])
    gate, up = gate_up[:, :hidden], gate_up[:, hidden:]
    down_t = ffn_all[:, 2 * hidden :]
    sigma = jax.nn.sigmoid(gate)
    active = (gate * sigma * up).astype(BF)
    d_active = dot(cot_all, down_t)
    d_gate = (d_active * up * sigma * (1.0 + gate * (1.0 - sigma))).astype(BF)
    d_up = (d_active * gate * sigma).astype(BF)
    d_gate_up = jnp.concatenate([d_gate, d_up], axis=1)
    d_second_part = dot(d_gate_up, ffn_all[:, : 2 * hidden], 1, 1).astype(BF)
    ffn_part = dot(active, down_t, 1, 1).astype(BF)
    d_second, ffn_out = exchange(
        5,
        (d_second_part.reshape(cols, tokens, width), "col", "s"),
        (ffn_part.reshape(cols, tokens, width), "col", "s"),
    )
    d_second = jnp.sum(d_second.astype(F32), axis=0)
    result = middle + jnp.sum(ffn_out.astype(F32), axis=0)
    ffn_grad = jnp.concatenate(
        [dot(normed2_all, d_gate_up, 0, 0), dot(cot_all, active, 0, 0)], axis=1
    ).astype(BF)

    second_back, gain2_grad = norm_back(middle, second_scale, gain2, d_second)
    d_middle = upstream + second_back
    d_attn = d_middle.astype(BF)
    d_attended = dot(d_attn, out_t).astype(BF)
    out_grad = dot(d_attn, attended, 0, 0)
    d_split = group_split(d_attended)
    row_dots = jnp.sum(d_split.astype(F32) * att_split, axis=2, keepdims=True)
    d_probs = jnp.einsum("gqd,gkd->gqk", d_split, values, preferred_element_type=F32)
    d_raw = (probs * (d_probs - row_dots) * soft_scale).astype(BF)
    d_query = group_merge(
        jnp.einsum("gqk,gkd->gqd", d_raw, keys, preferred_element_type=F32), tokens
    )
    d_key = jnp.einsum("gqk,gqd->kgd", d_raw, split_q, preferred_element_type=F32)
    d_value = jnp.einsum("gqk,gqd->kgd", probs_low, d_split, preferred_element_type=F32)
    d_kv = jnp.stack([d_key, d_value], axis=1).astype(BF)
    d_kv = d_kv.reshape(rows, cols * tokens, 2 * kv_width)
    d_kv_rows, ffn_rows = exchange(
        6, (d_kv, "row", "s"), (ffn_grad.reshape(rows, feat, 3 * hidden), "row", "s")
    )
    d_kv_sum = jnp.sum(d_kv_rows.astype(F32), axis=0).astype(BF)
    ffn_sum = jnp.sum(ffn_rows.astype(F32), axis=0).astype(BF)
    d_kv_cols, ffn_dp = exchange(
        7, (d_kv_sum.reshape(cols, tokens, 2 * kv_width), "col", "s"), (ffn_sum, "dp", "g")
    )
    d_kv_own = jnp.sum(d_kv_cols.astype(F32), axis=0)
    d_turned = rotate(jnp.concatenate([d_query, d_kv_own[:, :kv_width]], axis=1), cosine, -sine)
    d_qkv = jnp.concatenate([d_turned, d_kv_own[:, kv_width:]], axis=1).astype(BF)
    d_first = dot(d_qkv, qkv_weight, 1, 1)
    qkv_grad = dot(normed1, d_qkv, 0, 0)
    first_back, gain1_grad = norm_back(source, first_scale, gain1, d_first)
    input_grad_own = (d_middle + first_back).astype(BF)

    def by_col(grad):
        return grad.reshape(width, cols, grad.shape[1] // cols)

    qo_grad = jnp.concatenate(
        [
            by_col(qkv_grad[:, :width]),
            by_col(qkv_grad[:, width : width + kv_width]),
            by_col(qkv_grad[:, width + kv_width :]),
            by_col(out_grad),
        ],
        axis=2,
    ).astype(BF)
    qo_grad = qo_grad.reshape(rows, feat, cols, -1).transpose(0, 2, 1, 3)
    gain_grads = jnp.stack([gain1_grad, gain2_grad]).reshape(2, rows, feat).transpose(1, 0, 2)
    results = jnp.stack([result.astype(BF), input_grad_own])
    results = results.reshape(2, tokens, rows, feat).transpose(2, 1, 0, 3)
    results = results.reshape(rows, tokens, 2 * feat)
    qo_rows, gain_rows, result_rows = exchange(
        8, (qo_grad, "row", "s"), (gain_grads, "row", "s"), (results, "row", "s")
    )
    qo_sum = jnp.sum(qo_rows.astype(F32), axis=0).astype(BF)
    qo_cols_grad, gain_cols = exchange(
        9, (qo_sum, "col", "s"), (jnp.sum(gain_rows, axis=0), "col", "g")
    )
    qo_own = jnp.sum(qo_cols_grad.astype(F32), axis=0).astype(BF)
    qo_dp, gain_dp = exchange(10, (qo_own, "dp", "g"), (jnp.sum(gain_cols, axis=0), "dp", "g"))
    qo_final = jnp.sum(qo_dp.astype(F32), axis=0)
    ffn_final = jnp.sum(ffn_dp.astype(F32), axis=0)
    gain_final = jnp.sum(gain_dp, axis=0)
    result_rows = result_rows.reshape(block_tokens, 2 * feat)
    return (
        result_rows[:, :feat],
        result_rows[:, feat:],
        gain_final[0],
        qo_final[:, :q_cols],
        qo_final[:, q_cols : q_cols + k_cols],
        qo_final[:, q_cols + k_cols : q_cols + 2 * k_cols],
        qo_final[:, q_cols + 2 * k_cols :].T,
        gain_final[1],
        ffn_final[:, :hidden],
        ffn_final[:, hidden : 2 * hidden],
        ffn_final[:, 2 * hidden :].T,
    )


def solution(mesh):
    placed = (
        P(("dp", "col"), "row"),
        P("row"),
        P("row", "col"),
        P("row", "col"),
        P("row", "col"),
        P("col", "row"),
        P("row"),
        P("row", "col"),
        P("row", "col"),
        P("col", "row"),
        P(("dp", "col"), "row"),
    )
    return jax.shard_map(
        on_device,
        mesh=mesh,
        in_specs=placed,
        out_specs=(
            P(("dp", "col"), "row"),
            P(("dp", "col"), "row"),
            P("row"),
            P("row", "col"),
            P("row", "col"),
            P("row", "col"),
            P("col", "row"),
            P("row"),
            P("row", "col"),
            P("row", "col"),
            P("col", "row"),
        ),
        check_vma=False,
    )
```

time: 621 us -> 376 us (0.61)
  waiting for transfers between devices: 278 us -> 0 us
  Pallas kernels: 0 us -> 241 us
  blocking collectives: 227 us -> 0 us
  local copies, waits for them, and re-layouts: 25 us -> 50.2 us
  other arithmetic: 30.1 us -> 46 us
  between operations: 15 us -> 1.65 us
  starting transfers between devices: 13.1 us -> 0 us
    pallas_call x0 -> x11, Pallas kernels: none -> 241 us  [exchange(): pl.pallas_call(functools.partial(exchange_kernel, plan, axes), out_shape=...]
    all_gather x8 -> x0, blocking collectives: 163 us -> none  [the longest x4 65 us: rows_project(): gathered = lax.all_gather(values, 'col', axis=0, tiled=True)]
    reduce_scatter x8 -> x0, waiting for transfers between devices: 153 us -> none  [the longest x4 92.5 us: rows_project(): lax.psum_scatter(jnp.dot(gathered, weight, preferred_element_type=jnp.flo...]
    unnamed x13 -> x0, waiting for transfers between devices: 61.3 us -> none
    psum x6 -> x0, blocking collectives: 54.5 us -> none  [the longest x4 25.3 us: feature_sums(): return lax.psum(values, 'row')]
    all_gather x2 -> x0, waiting for transfers between devices: 33.4 us -> none  [cols_project(): gathered = lax.all_gather(values, 'row', axis=0, tiled=True)]
    all_to_all x3 -> x0, waiting for transfers between devices: 18 us -> none  [the longest x2 13.8 us: head_layout(): lax.all_to_all(values, 'col', split_axis=0, concat_axis=1, tiled=True)]
    all_to_all x3 -> x0, starting transfers between devices: 12.7 us -> none  [the longest x2 9.18 us: head_layout(): lax.all_to_all(values, 'col', split_axis=0, concat_axis=1, tiled=True)]
  transfers between devices with their start and end apart: 15 -> 0, of which waited for: 14 -> 0; matrix products, arithmetic and copies ran while one was open for 6% -> 0% of each run, Pallas kernels for 0% -> 0%
where the time goes in v1:
time: 376 us; the launch traced here: 375 us
  Pallas kernels  241 us (64%)
  local copies, waits for them, and re-layouts  50.2 us (13%)
  other arithmetic  46 us (12%)
  matrix products  35.4 us (9%)
    pallas_call x11, Pallas kernels, exchange(): pl.pallas_call(functools.partial(exchange_kernel, plan, axes), out_shape=...  241 us
    dot_general x12, matrix products, dot(): lax.dot_general(left, right, (((left_dim,), (right_dim,)), ((), ())), pre...  17 us
    unnamed x94, local copies, waits for them, and re-layouts  9.54 us
    sub x1, other arithmetic, on_device(): terms = jnp.exp(masked - top)  9.44 us

profile of v1, /device:TPU:0, one launch (start us, length us, event | category | flops | bytes accessed | tf_op | source)
XLA Modules:
  0.0 374.5 jit_solution(16995068168239945944)
XLA Ops:
  6.8 26.3 %exchange_0.1 = (bf16[4,128,288]{2,1,0:T(8,128)(2,1)}, f32[4,2,144]{2,1,0:T(2,128)}, bf16[4,144,1152]{2,1,0:T(8,128)(2,1)}, bf16[4,144,384]{2,1,0:T(8,128)(2,1)}) custom-call(bf16[4,128,288]{2,1,0:T(8,128)(2,1)} %bitcast.183, f32[2,144]{1,0:T(2,128)} %pad_maximum_fusion.16.refs_1_, bf16[144,1152]{1,0:T(8,128)(2,1)} %pad_maximum_fusion.9.refs_2_, ...), custom_call_target="tpu_custom_call" | custom-call | tf_op jit(solution)/shard_map/exchange_0/pallas_call | solution.py:77
  35.8 24.6 %exchange_1.1 = (bf16[4,4,144,384]{3,2,1,0:T(8,128)(2,1)}, bf16[4,128,576]{2,1,0:T(8,128)(2,1)}) custom-call(bf16[4,144,384]{2,1,0:T(8,128)(2,1)} %get-tuple-element.32.refs_0_, bf16[128,576]{1,0:T(8,128)(2,1)} %copy.191.refs_1_), custom_call_target="tpu_custom_call" | custom-call | tf_op jit(solution)/shard_map/exchange_1/pallas_call | solution.py:77
  71.3 11.3 %exchange_2.1.refs_0_ = bf16[4,128,384]{2,1,0:T(8,128)(2,1)} custom-call(bf16[128,384]{1,0:T(8,128)(2,1)} %pad_maximum_fusion.15.refs_0_), custom_call_target="tpu_custom_call" | custom-call | tf_op jit(solution)/shard_map/exchange_2/pallas_call | solution.py:77
  82.6 22.4 %exchange_3.1 = bf16[4,4,128,384]{3,2,1,0:T(8,128)(2,1)} custom-call(bf16[4,128,384]{2,1,0:T(8,128)(2,1)} %exchange_2.1.refs_0_), custom_call_target="tpu_custom_call" | custom-call | tf_op jit(solution)/shard_map/exchange_3/pallas_call | solution.py:77
  105.0 3.0 copy.206
  108.0 2.4 reshape.496
  111.2 2.6 fusion.13
  115.5 9.4 %fusion.82 = (f32[3,384]{1,0:T(4,128)S(1)}, f32[3,384,2048]{2,1,0:T(8,128)}) fusion(f32[3,384,2048]{2,1,0:T(8,128)S(1)} %fusion.13, pred[384,2048]{1,0:T(8,128)(4,1)} %compare_and_fusion), kind=kOutput, calls=%fused_computation.186 | output fusion | flops 14157823 | bytes 19665408 | tf_op jit(solution)/shard_map/sub | solution.py:218
  124.9 5.2 %fusion.5 = bf16[3,384,2048]{2,1,0:T(8,128)(2,1)S(1)} fusion(f32[3,384,2048]{2,1,0:T(8,128)} %get-tuple-element.138, f32[3,384]{1,0:T(4,128)S(1)} %get-tuple-element.137), kind=kLoop, calls=%fused_computation.9 | loop fusion | flops 4718592 | bytes 14160384 | tf_op jit(solution)/shard_map/convert_element_type | solution.py:221
  130.2 2.3 fusion.83
  135.5 18.2 %exchange_4.1 = bf16[4,128,576]{2,1,0:T(8,128)(2,1)} custom-call(bf16[128,576]{1,0:T(8,128)(2,1)} %multiply_convert_fusion.4.refs_0_), custom_call_target="tpu_custom_call" | custom-call | tf_op jit(solution)/shard_map/exchange_4/pallas_call | solution.py:77
  153.7 2.3 fusion.10
  159.2 2.1 copy.214
  161.3 2.3 convolution_convert_fusion.5
  163.6 2.1 copy.215
  165.7 33.8 %exchange_5.1 = (bf16[4,128,576]{2,1,0:T(8,128)(2,1)}, bf16[4,128,576]{2,1,0:T(8,128)(2,1)}) custom-call(bf16[4,128,576]{2,1,0:T(8,128)(2,1)} %bitcast.172, bf16[4,128,576]{2,1,0:T(8,128)(2,1)} %bitcast.173), custom_call_target="tpu_custom_call" | custom-call | tf_op jit(solution)/shard_map/exchange_5/pallas_call | solution.py:77
  204.8 2.4 convolution_convert_fusion.2
  207.9 3.3 fusion.7
  211.3 5.3 %multiply_convert_fusion = bf16[3,384,2048]{2,1,0:T(8,128)(2,1)S(1)} fusion(f32[3,384]{1,0:T(4,128)S(1)} %multiply_reduce_fusion.6, bf16[3,384,64]{1,2,0:T(8,128)(2,1)S(1)} %reshape.504, f32[3,384,2048]{2,1,0:T(8,128)} %get-tuple-element.138, f32[3,384]{1,0:T(4,128)S(1)} %get-tuple-element.137, bf16[2048,2,3,64]{0,3,2,1:T(8,128)(2,1)S(1)} %copy-done.2), kind=kOutput, calls=%fused_computation.1 | convolution fusion | flops 313786368 | bytes 15101952 | tf_op jit(solution)/shard_map/gqd,gkd->gqk/dot_general | solution.py:261
  218.9 2.4 convert_element_type.141
  221.3 4.0 %copy.222.refs_0_ = bf16[4,512,384]{2,1,0:T(8,128)(2,1)} copy(bf16[4,512,384]{1,0,2:T(4,128)(2,1)} %convert_element_type.141) | data formatting | bytes 3145728 | tf_op jit(solution)/shard_map/convert_element_type | solution.py:268
  226.7 2.3 convolution_convert_fusion.7
  230.0 2.0 convolution_convert_fusion.4
  233.2 35.8 %exchange_6.1 = (bf16[4,512,384]{2,1,0:T(8,128)(2,1)}, bf16[4,144,1152]{2,1,0:T(8,128)(2,1)}) custom-call(bf16[4,512,384]{2,1,0:T(8,128)(2,1)} %copy.222.refs_0_, bf16[4,144,1152]{2,1,0:T(8,128)(2,1)} %pad_maximum_fusion.1.refs_1_), custom_call_target="tpu_custom_call" | custom-call | tf_op jit(solution)/shard_map/exchange_6/pallas_call | solution.py:77
  269.1 2.6 reduce_sum.198
  272.7 17.4 %exchange_7.1 = (bf16[4,128,384]{2,1,0:T(8,128)(2,1)}, bf16[2,144,1152]{2,1,0:T(8,128)(2,1)}) custom-call(bf16[4,128,384]{2,1,0:T(8,128)(2,1)} %bitcast.184, bf16[144,1152]{1,0:T(8,128)(2,1)} %reduce_sum.199.refs_1_), custom_call_target="tpu_custom_call" | custom-call | tf_op jit(solution)/shard_map/exchange_7/pallas_call | solution.py:77
  291.3 3.9 %fusion.12 = f32[3,384,64]{1,2,0:T(8,128)S(1)} fusion(bf16[3,384,2048]{2,1,0:T(8,128)(2,1)} %copy-done.1, bf16[2048,2,3,64]{0,3,2,1:T(8,128)(2,1)S(1)} %copy-done.2), kind=kOutput, calls=%fused_computation.42 | convolution fusion | flops 301989888 | bytes 5799936 | tf_op jit(solution)/shard_map/gqk,gkd->gqd/dot_general | solution.py:264
  302.8 2.6 maximum_bitcast_fusion.refs_0_
  309.2 28.9 %exchange_8.1 = (bf16[4,4,144,384]{3,2,1,0:T(8,128)(2,1)}, f32[4,2,144]{2,1,0:T(2,128)}, bf16[4,128,288]{2,1,0:T(8,128)(2,1)}) custom-call(bf16[4,4,144,384]{3,2,1,0:T(8,128)(2,1)} %maximum_bitcast_fusion.refs_0_, f32[4,2,144]{2,1,0:T(2,128)} %maximum_bitcast_fusion.2.refs_1_, bf16[4,128,288]{2,1,0:T(8,128)(2,1)} %copy.242.refs_2_), custom_call_target="tpu_custom_call" | custom-call | tf_op jit(solution)/shard_map/exchange_8/pallas_call | solution.py:77
  342.7 16.1 %exchange_9.1 = (bf16[4,144,384]{2,1,0:T(8,128)(2,1)}, f32[4,2,144]{2,1,0:T(2,128)}) custom-call(bf16[4,144,384]{2,1,0:T(8,128)(2,1)} %reduce_sum.205.refs_0_, f32[2,144]{1,0:T(2,128)} %reduce_sum.206.refs_1_), custom_call_target="tpu_custom_call" | custom-call | tf_op jit(solution)/shard_map/exchange_9/pallas_call | solution.py:77
  358.9 1.8 reduce_sum.207.refs_0_
  361.9 6.4 %exchange_10.1 = (bf16[2,144,384]{2,1,0:T(8,128)(2,1)}, f32[2,2,144]{2,1,0:T(2,128)}) custom-call(bf16[144,384]{1,0:T(8,128)(2,1)} %reduce_sum.207.refs_0_, f32[2,144]{1,0:T(2,128)} %reduce_sum.208.refs_1_), custom_call_target="tpu_custom_call" | custom-call | tf_op jit(solution)/shard_map/exchange_10/pallas_call | solution.py:77
  (203 shorter events, 65.3 us)
Async XLA Ops:
  0.6 5.1 %copy-start.31 = (bf16[144,144]{1,0:T(8,128)(2,1)S(1)}, bf16[144,144]{1,0:T(8,128)(2,1)}, u32[]{:S(2)}) copy-start(bf16[144,144]{1,0:T(8,128)(2,1)} %param.16) | copy-start | bytes 124420
  0.7 5.2 %copy-start.33 = (bf16[144,48]{0,1:T(8,128)(2,1)S(1)}, bf16[144,48]{0,1:T(8,128)(2,1)}, u32[]{:S(2)}) copy-start(bf16[144,48]{0,1:T(8,128)(2,1)} %param.15) | copy-start | bytes 41476
  0.7 5.3 %copy-start.34 = (bf16[144,48]{0,1:T(8,128)(2,1)S(1)}, bf16[144,48]{0,1:T(8,128)(2,1)}, u32[]{:S(2)}) copy-start(bf16[144,48]{0,1:T(8,128)(2,1)} %param.14) | copy-start | bytes 41476
  0.7 5.4 %copy-start.32 = (bf16[144,144]{1,0:T(8,128)(2,1)S(1)}, bf16[144,144]{1,0:T(8,128)(2,1)}, u32[]{:S(2)}) copy-start(bf16[144,144]{1,0:T(8,128)(2,1)} %param.13) | copy-start | bytes 124420
  65.7 1.7 copy-start.28
  65.7 1.7 copy-start.29
  66.4 1.6 copy-start.23
  70.2 12.3 %copy-start.5 = (f32[128,768]{1,0:T(8,128)}, f32[128,768]{1,0:T(8,128)S(1)}, u32[]{:S(2)}) copy-start(f32[128,768]{1,0:T(8,128)S(1)} %copy.197) | copy-start | bytes 1179652
  124.9 5.2 %copy-start.2 = (bf16[2048,2,3,64]{0,3,2,1:T(8,128)(2,1)S(1)}, bf16[2048,2,3,64]{0,3,2,1:T(8,128)(2,1)}, u32[]{:S(2)}) copy-start(bf16[2048,2,3,64]{0,3,2,1:T(8,128)(2,1)} %reshape.496) | copy-start | bytes 4718596
  130.2 2.3 copy-start
  132.6 3.0 copy-start.19
  153.7 2.4 copy-start.17
  153.7 2.4 copy-start.26
  156.9 4.4 %copy-start.15 = (bf16[512,384]{0,1:T(8,128)(2,1)}, bf16[512,384]{0,1:T(8,128)(2,1)S(1)}, u32[]{:S(2)}) copy-start(bf16[512,384]{0,1:T(8,128)(2,1)S(1)} %get-tuple-element.107) | copy-start | bytes 1179652
  199.5 3.3 copy-start.16
  203.6 4.3 %copy-start.7 = (f32[128,576]{1,0:T(8,128)}, f32[128,576]{1,0:T(8,128)S(1)}, u32[]{:S(2)}) copy-start(f32[128,576]{1,0:T(8,128)S(1)} %get-tuple-element.100) | copy-start | bytes 884740
  207.9 3.4 copy-start.20
  211.3 5.3 %copy-start.11 = (bf16[128,576]{0,1:T(8,128)(2,1)S(1)}, bf16[128,576]{0,1:T(8,128)(2,1)}, u32[]{:S(2)}) copy-start(bf16[128,576]{0,1:T(8,128)(2,1)} %copy.203) | copy-start | bytes 442372
  216.6 2.2 copy-start.1
  225.3 3.6 copy-start.3
  230.0 2.0 copy-start.13
  269.0 2.6 copy-start.18
  300.7 1.3 copy-start.4
  301.5 1.3 copy-start.10
  302.8 2.7 copy-start.22
  302.8 2.7 copy-start.24
  305.5 2.3 copy-start.8
  305.5 2.3 copy-start.37
  305.5 2.6 copy-start.27
  338.1 2.9 copy-start.12
  339.5 2.7 copy-start.36
  342.1 31.4 %copy-start.25 = (bf16[2,144,1152]{2,1,0:T(8,128)(2,1)S(1)}, bf16[2,144,1152]{2,1,0:T(8,128)(2,1)}, u32[]{:S(2)}) copy-start(bf16[2,144,1152]{2,1,0:T(8,128)(2,1)} %get-tuple-element.48) | copy-start | bytes 1990660
  (8 other events, 7.0 us)

commit v2 on v1

--- a/solution.py
+++ b/solution.py
@@ -36,12 +36,18 @@
     pl.semaphore_wait(barrier, total)
     sizes = dict(axes)
     copies = []
+    relays = []
     for item, (axis, mode) in enumerate(plan):
         size = sizes[axis]
         me = lax.axis_index(axis)
+        near = me + 1 - 2 * lax.rem(me, 2)
         for step in range(1, size):
             peer = lax.rem(me + step, size)
-            source = ins[item] if mode == "g" else ins[item].at[peer]
+            if mode == "r":
+                if step == 3:
+                    continue
+                peer = near if step == 1 else lax.rem(me + 2, size)
+            source = ins[item].at[peer] if mode == "s" else ins[item]
             copy = pltpu.make_async_remote_copy(
                 src_ref=source,
                 dst_ref=outs[item].at[me],
@@ -51,25 +57,46 @@
                 device_id_type=MESH,
             )
             copy.start()
-            copies.append(copy)
+            if mode == "r" and step == 2:
+                relays.append((item, axis, peer, near, copy))
+            else:
+                copies.append(copy)
     for item, (axis, mode) in enumerate(plan):
         me = lax.axis_index(axis)
-        source = ins[item] if mode == "g" else ins[item].at[me]
+        source = ins[item].at[me] if mode == "s" else ins[item]
         copy = pltpu.make_async_copy(source, outs[item].at[me], local_sem.at[item])
         copy.start()
         copies.append(copy)
+    for item, axis, across, near, arrived in relays:
+        arrived.wait_recv()
+        copy = pltpu.make_async_remote_copy(
+            src_ref=outs[item].at[across],
+            dst_ref=outs[item].at[across],
+            send_sem=send_sem.at[item, 3],
+            recv_sem=recv_sem.at[item, 3],
+            device_id={axis: near},
+            device_id_type=MESH,
+        )
+        copy.start()
+        copies.append(copy)
+    for _, _, _, _, arrived in relays:
+        arrived.wait_send()
     for copy in copies:
         copy.wait()
 
 
 def exchange(ident, *items):
+    items = [
+        (array, axis, "r" if mode == "g" and axis == "row" and lax.axis_size(axis) == 4 else mode)
+        for array, axis, mode in items
+    ]
     plan = tuple((axis, mode) for _, axis, mode in items)
     axes = tuple((axis, lax.axis_size(axis)) for axis in dict.fromkeys(a for a, _ in plan))
     arrays = [array for array, _, _ in items]
     widest = max(size for _, size in axes)
     out_shape = tuple(
         jax.ShapeDtypeStruct(
-            ((lax.axis_size(axis),) + array.shape) if mode == "g" else array.shape, array.dtype
+            array.shape if mode == "s" else ((lax.axis_size(axis),) + array.shape), array.dtype
         )
         for array, axis, mode in items
     )
@@ -159,12 +186,8 @@
     qo_block = jnp.concatenate([query_weight, key_matrix, value_matrix, output_weight.T], axis=1)
     joint = jnp.concatenate([inputs, cotangent], axis=1).reshape(rows, tokens, 2 * feat)
     gains = jnp.stack([first_gain, second_gain])
-    joint_all, gain_all, ffn_all, qo_cols = exchange(
-        0,
-        (joint, "row", "s"),
-        (gains, "row", "g"),
-        (ffn_block, "row", "g"),
-        (qo_block, "col", "g"),
+    joint_all, gain_all, qo_cols = exchange(
+        0, (joint, "row", "s"), (gains, "row", "g"), (qo_block, "col", "g")
     )
     joint_all = joint_all.transpose(1, 0, 2)
     source = joint_all[:, :, :feat].reshape(tokens, width).astype(F32)
@@ -225,7 +248,7 @@
     second_scale = norm_scale(middle)
     normed2 = (middle * second_scale * gain2).astype(BF)
 
-    (normed2_all,) = exchange(4, (normed2, "col", "g"))
+    normed2_all, ffn_all = exchange(4, (normed2, "col", "g"), (ffn_block, "row", "g"))
     normed2_all = normed2_all.reshape(cols * tokens, width)
     cot_all = cot_all.reshape(cols * tokens, width)
     ffn_all = ffn_all.reshape(width, 3 * hidden)
@@ -240,16 +263,16 @@
     d_gate_up = jnp.concatenate([d_gate, d_up], axis=1)
     d_second_part = dot(d_gate_up, ffn_all[:, : 2 * hidden], 1, 1).astype(BF)
     ffn_part = dot(active, down_t, 1, 1).astype(BF)
-    d_second, ffn_out = exchange(
-        5,
-        (d_second_part.reshape(cols, tokens, width), "col", "s"),
-        (ffn_part.reshape(cols, tokens, width), "col", "s"),
-    )
-    d_second = jnp.sum(d_second.astype(F32), axis=0)
-    result = middle + jnp.sum(ffn_out.astype(F32), axis=0)
     ffn_grad = jnp.concatenate(
         [dot(normed2_all, d_gate_up, 0, 0), dot(cot_all, active, 0, 0)], axis=1
     ).astype(BF)
+    d_second, ffn_rows = exchange(
+        5,
+        (d_second_part.reshape(cols, tokens, width), "col", "s"),
+        (ffn_grad.reshape(rows, feat, 3 * hidden), "row", "s"),
+    )
+    d_second = jnp.sum(d_second.astype(F32), axis=0)
+    ffn_sum = jnp.sum(ffn_rows.astype(F32), axis=0).astype(BF)
 
     second_back, gain2_grad = norm_back(middle, second_scale, gain2, d_second)
     d_middle = upstream + second_back
@@ -267,14 +290,26 @@
     d_value = jnp.einsum("gqk,gqd->kgd", probs_low, d_split, preferred_element_type=F32)
     d_kv = jnp.stack([d_key, d_value], axis=1).astype(BF)
     d_kv = d_kv.reshape(rows, cols * tokens, 2 * kv_width)
-    d_kv_rows, ffn_rows = exchange(
-        6, (d_kv, "row", "s"), (ffn_grad.reshape(rows, feat, 3 * hidden), "row", "s")
+    d_kv_rows, ffn_out, ffn_dp = exchange(
+        6,
+        (d_kv, "row", "s"),
+        (ffn_part.reshape(cols, tokens, width), "col", "s"),
+        (ffn_sum, "dp", "g"),
     )
     d_kv_sum = jnp.sum(d_kv_rows.astype(F32), axis=0).astype(BF)
-    ffn_sum = jnp.sum(ffn_rows.astype(F32), axis=0).astype(BF)
-    d_kv_cols, ffn_dp = exchange(
-        7, (d_kv_sum.reshape(cols, tokens, 2 * kv_width), "col", "s"), (ffn_sum, "dp", "g")
-    )
+    result = (middle + jnp.sum(ffn_out.astype(F32), axis=0)).astype(BF)
+
+    def by_row(own):
+        return own.reshape(tokens, rows, feat).transpose(1, 0, 2)
+
+    d_kv_cols, out_rows, result_rows = exchange(
+        7,
+        (d_kv_sum.reshape(cols, tokens, 2 * kv_width), "col", "s"),
+        (out_grad.astype(BF).reshape(rows, feat, width), "row", "s"),
+        (by_row(result), "row", "s"),
+    )
+    out_sum = jnp.sum(out_rows.astype(F32), axis=0).astype(BF)
+    out_sum = out_sum.reshape(feat, cols, q_cols).transpose(1, 0, 2)
     d_kv_own = jnp.sum(d_kv_cols.astype(F32), axis=0)
     d_turned = rotate(jnp.concatenate([d_query, d_kv_own[:, :kv_width]], axis=1), cosine, -sine)
     d_qkv = jnp.concatenate([d_turned, d_kv_own[:, kv_width:]], axis=1).astype(BF)
@@ -283,44 +318,44 @@
     first_back, gain1_grad = norm_back(source, first_scale, gain1, d_first)
     input_grad_own = (d_middle + first_back).astype(BF)
 
-    def by_col(grad):
-        return grad.reshape(width, cols, grad.shape[1] // cols)
-
-    qo_grad = jnp.concatenate(
+    gain_grads = jnp.stack([gain1_grad, gain2_grad]).reshape(2, rows, feat).transpose(1, 0, 2)
+    qkv_rows, gain_rows, input_rows, out_cols = exchange(
+        8,
+        (qkv_grad.astype(BF).reshape(rows, feat, width + 2 * kv_width), "row", "s"),
+        (gain_grads, "row", "s"),
+        (by_row(input_grad_own), "row", "s"),
+        (out_sum, "col", "s"),
+    )
+    qkv_sum = jnp.sum(qkv_rows.astype(F32), axis=0).astype(BF)
+    qkv_sum = jnp.concatenate(
         [
-            by_col(qkv_grad[:, :width]),
-            by_col(qkv_grad[:, width : width + kv_width]),
-            by_col(qkv_grad[:, width + kv_width :]),
-            by_col(out_grad),
+            qkv_sum[:, :width].reshape(feat, cols, q_cols),
+            qkv_sum[:, width : width + kv_width].reshape(feat, cols, k_cols),
+            qkv_sum[:, width + kv_width :].reshape(feat, cols, k_cols),
         ],
         axis=2,
-    ).astype(BF)
-    qo_grad = qo_grad.reshape(rows, feat, cols, -1).transpose(0, 2, 1, 3)
-    gain_grads = jnp.stack([gain1_grad, gain2_grad]).reshape(2, rows, feat).transpose(1, 0, 2)
-    results = jnp.stack([result.astype(BF), input_grad_own])
-    results = results.reshape(2, tokens, rows, feat).transpose(2, 1, 0, 3)
-    results = results.reshape(rows, tokens, 2 * feat)
-    qo_rows, gain_rows, result_rows = exchange(
-        8, (qo_grad, "row", "s"), (gain_grads, "row", "s"), (results, "row", "s")
-    )
-    qo_sum = jnp.sum(qo_rows.astype(F32), axis=0).astype(BF)
-    qo_cols_grad, gain_cols = exchange(
-        9, (qo_sum, "col", "s"), (jnp.sum(gain_rows, axis=0), "col", "g")
-    )
-    qo_own = jnp.sum(qo_cols_grad.astype(F32), axis=0).astype(BF)
-    qo_dp, gain_dp = exchange(10, (qo_own, "dp", "g"), (jnp.sum(gain_cols, axis=0), "dp", "g"))
-    qo_final = jnp.sum(qo_dp.astype(F32), axis=0)
+    ).transpose(1, 0, 2)
+    out_own = jnp.sum(out_cols.astype(F32), axis=0).astype(BF)
+    qkv_cols, gain_cols, out_dp = exchange(
+        9,
+        (qkv_sum, "col", "s"),
+        (jnp.sum(gain_rows, axis=0), "col", "g"),
+        (out_own, "dp", "g"),
+    )
+    qkv_own = jnp.sum(qkv_cols.astype(F32), axis=0).astype(BF)
+    qkv_dp, gain_dp = exchange(10, (qkv_own, "dp", "g"), (jnp.sum(gain_cols, axis=0), "dp", "g"))
+    qkv_final = jnp.sum(qkv_dp.astype(F32), axis=0)
+    out_final = jnp.sum(out_dp.astype(F32), axis=0)
     ffn_final = jnp.sum(ffn_dp.astype(F32), axis=0)
     gain_final = jnp.sum(gain_dp, axis=0)
-    result_rows = result_rows.reshape(block_tokens, 2 * feat)
     return (
-        result_rows[:, :feat],
-        result_rows[:, feat:],
+        result_rows.reshape(block_tokens, feat),
+        input_rows.reshape(block_tokens, feat),
         gain_final[0],
-        qo_final[:, :q_cols],
-        qo_final[:, q_cols : q_cols + k_cols],
-        qo_final[:, q_cols + k_cols : q_cols + 2 * k_cols],
-        qo_final[:, q_cols + 2 * k_cols :].T,
+        qkv_final[:, :q_cols],
+        qkv_final[:, q_cols : q_cols + k_cols],
+        qkv_final[:, q_cols + k_cols :],
+        out_final.T,
         gain_final[1],
         ffn_final[:, :hidden],
         ffn_final[:, hidden : 2 * hidden],

time: 376 us -> 320 us (0.85)
  Pallas kernels: 241 us -> 185 us
    pallas_call x11, Pallas kernels: 241 us -> 185 us  [exchange(): pl.pallas_call(functools.partial(exchange_kernel, plan, axes), out_shape=...]
    unnamed x94 -> x88, local copies, waits for them, and re-layouts: 9.54 us -> 12.1 us
where the time goes in v2:
time: 320 us; the launch traced here: 319 us
  Pallas kernels  185 us (58%)
  local copies, waits for them, and re-layouts  52.6 us (16%)
  other arithmetic  44.8 us (14%)
  matrix products  34.3 us (11%)
    pallas_call x11, Pallas kernels, exchange(): pl.pallas_call(functools.partial(exchange_kernel, plan, axes), out_shape=...  185 us
    dot_general x12, matrix products, dot(): lax.dot_general(left, right, (((left_dim,), (right_dim,)), ((), ())), pre...  15.9 us
    unnamed x88, local copies, waits for them, and re-layouts  12.1 us
    sub x1, other arithmetic, on_device(): terms = jnp.exp(masked - top)  9.47 us
    slice x6, local copies, waits for them, and re-layouts, on_device(): parts.append(qo_all[:, :, at:at + size].reshape(width, cols * size))  8.55 us

profile of v2, /device:TPU:0, one launch (start us, length us, event | category | flops | bytes accessed | tf_op | source)
XLA Modules:
  0.0 318.7 jit_solution(14126467219697627640)
XLA Ops:
  8.2 16.5 %exchange_0.1 = (bf16[4,128,288]{2,1,0:T(8,128)(2,1)}, f32[4,2,144]{2,1,0:T(2,128)}, bf16[4,144,384]{2,1,0:T(8,128)(2,1)}) custom-call(bf16[4,128,288]{2,1,0:T(8,128)(2,1)} %bitcast.179, f32[2,144]{1,0:T(2,128)} %pad_maximum_fusion.16.refs_1_, bf16[144,384]{1,0:T(8,128)(2,1)} %pad_maximum_fusion.14.refs_2_), custom_call_target="tpu_custom_call" | custom-call | tf_op jit(solution)/shard_map/exchange_0/pallas_call | solution.py:104
  26.9 18.9 %exchange_1.1 = (bf16[4,4,144,384]{3,2,1,0:T(8,128)(2,1)}, bf16[4,128,576]{2,1,0:T(8,128)(2,1)}) custom-call(bf16[4,144,384]{2,1,0:T(8,128)(2,1)} %get-tuple-element.37.refs_0_, bf16[128,576]{1,0:T(8,128)(2,1)} %copy.187.refs_1_), custom_call_target="tpu_custom_call" | custom-call | tf_op jit(solution)/shard_map/exchange_1/pallas_call | solution.py:104
  49.0 2.2 copy.205
  61.7 12.4 %exchange_2.1.refs_0_ = bf16[4,128,384]{2,1,0:T(8,128)(2,1)} custom-call(bf16[128,384]{1,0:T(8,128)(2,1)} %pad_maximum_fusion.15.refs_0_), custom_call_target="tpu_custom_call" | custom-call | tf_op jit(solution)/shard_map/exchange_2/pallas_call | solution.py:104
  74.1 15.0 %exchange_3.1 = bf16[4,4,128,384]{3,2,1,0:T(8,128)(2,1)} custom-call(bf16[4,128,384]{2,1,0:T(8,128)(2,1)} %exchange_2.1.refs_0_), custom_call_target="tpu_custom_call" | custom-call | tf_op jit(solution)/shard_map/exchange_3/pallas_call | solution.py:104
  89.1 3.0 copy.202
  92.1 2.4 reshape.498
  95.3 2.6 fusion.13
  99.6 9.5 %fusion.82 = (f32[3,384]{1,0:T(4,128)S(1)}, f32[3,384,2048]{2,1,0:T(8,128)}) fusion(f32[3,384,2048]{2,1,0:T(8,128)S(1)} %fusion.13, pred[384,2048]{1,0:T(8,128)(4,1)} %compare_and_fusion), kind=kOutput, calls=%fused_computation.185 | output fusion | flops 14157823 | bytes 19665408 | tf_op jit(solution)/shard_map/sub | solution.py:241
  109.0 5.2 %fusion.5 = bf16[3,384,2048]{2,1,0:T(8,128)(2,1)S(1)} fusion(f32[3,384,2048]{2,1,0:T(8,128)} %get-tuple-element.141, f32[3,384]{1,0:T(4,128)S(1)} %get-tuple-element.140), kind=kLoop, calls=%fused_computation.9 | loop fusion | flops 4718592 | bytes 14160384 | tf_op jit(solution)/shard_map/convert_element_type | solution.py:244
  114.3 2.3 fusion.83
  118.0 1.7 pad_maximum_fusion.9.refs_1_
  119.7 19.1 %exchange_4.1 = (bf16[4,128,576]{2,1,0:T(8,128)(2,1)}, bf16[4,144,1152]{2,1,0:T(8,128)(2,1)}) custom-call(bf16[128,576]{1,0:T(8,128)(2,1)} %multiply_convert_fusion.4.refs_0_, bf16[144,1152]{1,0:T(8,128)(2,1)} %pad_maximum_fusion.9.refs_1_), custom_call_target="tpu_custom_call" | custom-call | tf_op jit(solution)/shard_map/exchange_4/pallas_call | solution.py:104
  138.9 2.3 fusion.10
  145.1 2.2 copy.210
  147.3 2.1 copy.213
  149.4 2.5 convolution_convert_fusion.7
  153.0 2.0 convolution_convert_fusion.3
  156.1 22.8 %exchange_5.1 = (bf16[4,128,576]{2,1,0:T(8,128)(2,1)}, bf16[4,144,1152]{2,1,0:T(8,128)(2,1)}) custom-call(bf16[4,128,576]{2,1,0:T(8,128)(2,1)} %bitcast.166, bf16[4,144,1152]{2,1,0:T(8,128)(2,1)} %pad_maximum_fusion.1.refs_1_), custom_call_target="tpu_custom_call" | custom-call | tf_op jit(solution)/shard_map/exchange_5/pallas_call | solution.py:104
  181.5 3.3 %fusion.7 = bf16[2048,1,3,64]{0,3,2,1:T(8,128)(2,1)S(1)} fusion(bf16[3,384,64]{1,2,0:T(8,128)(2,1)S(1)} %reshape.505, bf16[3,384,2048]{2,1,0:T(8,128)(2,1)} %copy-done), kind=kOutput, calls=%fused_computation.14 | convolution fusion | flops 302383104 | bytes 5652480 | tf_op jit(solution)/shard_map/gqk,gqd->kgd/dot_general | solution.py:290
  184.9 5.3 %multiply_convert_fusion = bf16[3,384,2048]{2,1,0:T(8,128)(2,1)S(1)} fusion(f32[3,384]{1,0:T(4,128)S(1)} %multiply_reduce_fusion.6, bf16[3,384,64]{1,2,0:T(8,128)(2,1)S(1)} %reshape.505, f32[3,384,2048]{2,1,0:T(8,128)} %get-tuple-element.141, f32[3,384]{1,0:T(4,128)S(1)} %get-tuple-element.140, bf16[2048,2,3,64]{0,3,2,1:T(8,128)(2,1)S(1)} %copy-done.2), kind=kOutput, calls=%fused_computation.1 | convolution fusion | flops 313786368 | bytes 15101952 | tf_op jit(solution)/shard_map/gqd,gkd->gqk/dot_general | solution.py:284
  192.5 2.4 convert_element_type.151
  194.9 4.0 %copy.217.refs_0_ = bf16[4,512,384]{2,1,0:T(8,128)(2,1)} copy(bf16[4,512,384]{1,0,2:T(4,128)(2,1)} %convert_element_type.151) | data formatting | bytes 3145728 | tf_op jit(solution)/shard_map/convert_element_type | solution.py:291
  201.4 2.3 reduce_sum.231.refs_2_
  203.7 23.8 %exchange_6.1 = (bf16[4,512,384]{2,1,0:T(8,128)(2,1)}, bf16[4,128,576]{2,1,0:T(8,128)(2,1)}, bf16[2,144,1152]{2,1,0:T(8,128)(2,1)}) custom-call(bf16[4,512,384]{2,1,0:T(8,128)(2,1)} %copy.217.refs_0_, bf16[4,128,576]{2,1,0:T(8,128)(2,1)} %bitcast.165, bf16[144,1152]{1,0:T(8,128)(2,1)} %reduce_sum.231.refs_2_), custom_call_target="tpu_custom_call" | custom-call | tf_op jit(solution)/shard_map/exchange_6/pallas_call | solution.py:104
  227.6 2.5 reduce_sum.232
  232.5 16.3 %exchange_7.1 = (bf16[4,128,384]{2,1,0:T(8,128)(2,1)}, bf16[4,144,576]{2,1,0:T(8,128)(2,1)}, bf16[4,128,144]{2,1,0:T(8,128)(2,1)}) custom-call(bf16[4,128,384]{2,1,0:T(8,128)(2,1)} %bitcast.178, bf16[4,144,576]{2,1,0:T(8,128)(2,1)} %bitcast.164, bf16[4,128,144]{2,1,0:T(8,128)(2,1)} %bitcast.191), custom_call_target="tpu_custom_call" | custom-call | tf_op jit(solution)/shard_map/exchange_7/pallas_call | solution.py:104
  248.9 1.7 copy.239
  251.8 3.9 %fusion.12 = f32[3,384,64]{1,2,0:T(8,128)S(1)} fusion(bf16[3,384,2048]{2,1,0:T(8,128)(2,1)} %copy-done.1, bf16[2048,2,3,64]{0,3,2,1:T(8,128)(2,1)S(1)} %copy-done.2), kind=kOutput, calls=%fused_computation.41 | convolution fusion | flops 301989888 | bytes 5799936 | tf_op jit(solution)/shard_map/gqk,gkd->gqd/dot_general | solution.py:287
  262.4 21.8 %exchange_8.1 = (bf16[4,144,960]{2,1,0:T(8,128)(2,1)}, f32[4,2,144]{2,1,0:T(2,128)}, bf16[4,128,144]{2,1,0:T(8,128)(2,1)}, bf16[4,144,144]{2,1,0:T(8,128)(2,1)}) custom-call(bf16[4,144,960]{2,1,0:T(8,128)(2,1)} %bitcast.163, f32[4,2,144]{2,1,0:T(2,128)} %maximum_bitcast_fusion.1.refs_1_, bf16[4,128,144]{2,1,0:T(8,128)(2,1)} %bitcast.190, ...), custom_call_target="tpu_custom_call" | custom-call | tf_op jit(solution)/shard_map/exchange_8/pallas_call | solution.py:104
  290.5 12.8 %exchange_9.1 = (bf16[4,144,240]{2,1,0:T(8,128)(2,1)}, f32[4,2,144]{2,1,0:T(2,128)}, bf16[2,144,144]{2,1,0:T(8,128)(2,1)}) custom-call(bf16[4,144,240]{2,1,0:T(8,128)(2,1)} %maximum_bitcast_fusion.refs_0_, f32[2,144]{1,0:T(2,128)} %reduce_sum.240.refs_1_, bf16[144,144]{1,0:T(8,128)(2,1)} %reduce_sum.241.refs_2_), custom_call_target="tpu_custom_call" | custom-call | tf_op jit(solution)/shard_map/exchange_9/pallas_call | solution.py:104
  306.3 6.0 %exchange_10.1 = (bf16[2,144,240]{2,1,0:T(8,128)(2,1)}, f32[2,2,144]{2,1,0:T(2,128)}) custom-call(bf16[144,240]{1,0:T(8,128)(2,1)} %reduce_sum.242.refs_0_, f32[2,144]{1,0:T(2,128)} %reduce_sum.243.refs_1_), custom_call_target="tpu_custom_call" | custom-call | tf_op jit(solution)/shard_map/exchange_10/pallas_call | solution.py:104
  (199 shorter events, 66.2 us)
Async XLA Ops:
  53.3 63.4 %copy-start.4 = (f32[128,576]{1,0:T(8,128)}, f32[128,576]{1,0:T(8,128)S(1)}, u32[]{:S(2)}) copy-start(f32[128,576]{1,0:T(8,128)S(1)} %copy.185) | copy-start | bytes 884740
  54.7 3.4 %copy-start.33 = (f32[4,2,144]{2,1,0:T(2,128)S(1)}, f32[4,2,144]{2,1,0:T(2,128)}, u32[]{:S(2)}) copy-start(f32[4,2,144]{2,1,0:T(2,128)} %get-tuple-element.36) | copy-start | bytes 13828
  54.7 3.5 %copy-start.13 = (bf16[4,128,288]{2,1,0:T(8,128)(2,1)S(1)}, bf16[4,128,288]{2,1,0:T(8,128)(2,1)}, u32[]{:S(2)}) copy-start(bf16[4,128,288]{2,1,0:T(8,128)(2,1)} %get-tuple-element.35) | copy-start | bytes 884740
  56.1 2.9 copy-start.28
  57.5 1.5 copy-start.30
  60.6 13.4 %copy-start.8 = (f32[128,768]{1,0:T(8,128)}, f32[128,768]{1,0:T(8,128)S(1)}, u32[]{:S(2)}) copy-start(f32[128,768]{1,0:T(8,128)S(1)} %copy.193) | copy-start | bytes 1179652
  109.0 5.2 %copy-start.2 = (bf16[2048,2,3,64]{0,3,2,1:T(8,128)(2,1)S(1)}, bf16[2048,2,3,64]{0,3,2,1:T(8,128)(2,1)}, u32[]{:S(2)}) copy-start(bf16[2048,2,3,64]{0,3,2,1:T(8,128)(2,1)} %reshape.498) | copy-start | bytes 4718596
  114.3 2.3 copy-start
  114.3 2.4 copy-start.3
  116.6 1.4 copy-start.32
  116.6 24.5 %copy-start.17 = (bf16[128,3,3,64]{0,3,2,1:T(8,128)(2,1)}, bf16[128,3,3,64]{0,3,2,1:T(8,128)(2,1)S(1)}, u32[]{:S(2)}) copy-start(bf16[128,3,3,64]{0,3,2,1:T(8,128)(2,1)S(1)} %copy.204) | copy-start | bytes 442372
  119.7 21.5 %copy-start.24 = (bf16[4,128,576]{2,1,0:T(8,128)(2,1)S(1)}, bf16[4,128,576]{2,1,0:T(8,128)(2,1)}, u32[]{:S(2)}) copy-start(bf16[4,128,576]{2,1,0:T(8,128)(2,1)} %get-tuple-element.39) | copy-start | bytes 1769476
  138.8 2.3 copy-start.16
  145.1 6.8 %copy-start.10 = (bf16[4,128,576]{2,1,0:T(8,128)(2,1)S(1)}, bf16[4,128,576]{2,1,0:T(8,128)(2,1)}, u32[]{:S(2)}) copy-start(bf16[4,128,576]{2,1,0:T(8,128)(2,1)} %get-tuple-element.41) | copy-start | bytes 1769476
  153.0 2.0 copy-start.12
  156.1 24.2 %copy-start.15 = (bf16[128,576]{1,0:T(8,128)(2,1)S(1)}, bf16[128,576]{1,0:T(8,128)(2,1)}, u32[]{:S(2)}) copy-start(bf16[128,576]{1,0:T(8,128)(2,1)} %copy.187.refs_1_) | copy-start | bytes 442372
  181.5 3.4 %copy-start.19 = (f32[3,384,64]{1,2,0:T(8,128)S(1)}, f32[3,384,64]{1,2,0:T(8,128)}, u32[]{:S(2)}) copy-start(f32[3,384,64]{1,2,0:T(8,128)} %get-tuple-element.143) | copy-start | bytes 884740
  184.9 5.3 %copy-start.11 = (bf16[128,576]{0,1:T(8,128)(2,1)S(1)}, bf16[128,576]{0,1:T(8,128)(2,1)}, u32[]{:S(2)}) copy-start(bf16[128,576]{0,1:T(8,128)(2,1)} %copy.199) | copy-start | bytes 442372
  190.2 2.1 copy-start.1
  194.8 4.0 %copy-start.14 = (bf16[512,384]{0,1:T(8,128)(2,1)S(1)}, bf16[512,384]{0,1:T(8,128)(2,1)}, u32[]{:S(2)}) copy-start(bf16[512,384]{0,1:T(8,128)(2,1)} %get-tuple-element.115) | copy-start | bytes 1179652
  203.7 26.4 %copy-start.7 = (f32[128,576]{1,0:T(8,128)S(1)}, f32[128,576]{1,0:T(8,128)}, u32[]{:S(2)}) copy-start(f32[128,576]{1,0:T(8,128)} %copy-done.6) | copy-start | bytes 884740
  203.7 26.4 %copy-start.18 = (bf16[128,3,3,64]{0,3,2,1:T(8,128)(2,1)S(1)}, bf16[128,3,3,64]{0,3,2,1:T(8,128)(2,1)}, u32[]{:S(2)}) copy-start(bf16[128,3,3,64]{0,3,2,1:T(8,128)(2,1)} %copy-done.17) | copy-start | bytes 442372
  227.6 3.8 %copy-start.25 = (bf16[4,128,576]{2,1,0:T(8,128)(2,1)S(1)}, bf16[4,128,576]{2,1,0:T(8,128)(2,1)}, u32[]{:S(2)}) copy-start(bf16[4,128,576]{2,1,0:T(8,128)(2,1)} %get-tuple-element.45) | copy-start | bytes 1769476
  256.2 1.0 copy-start.5
  256.8 2.1 copy-start.29
  256.8 2.1 copy-start.31
  257.2 1.7 copy-start.22
  259.4 1.9 copy-start.20
  287.4 1.8 copy-start.34
  287.4 2.4 copy-start.27
  288.4 29.4 %copy-start.23 = (bf16[2,144,1152]{2,1,0:T(8,128)(2,1)S(1)}, bf16[2,144,1152]{2,1,0:T(8,128)(2,1)}, u32[]{:S(2)}) copy-start(bf16[2,144,1152]{2,1,0:T(8,128)(2,1)} %get-tuple-element.58) | copy-start | bytes 1990660
  314.5 4.2 %copy-start.26 = (f32[144,240]{1,0:T(8,128)}, f32[144,240]{1,0:T(8,128)S(1)}, u32[]{:S(2)}) copy-start(f32[144,240]{1,0:T(8,128)S(1)} %convert_reduce_fusion.5) | copy-start | bytes 414724
  (5 other events, 4.3 us)
